TPU v7x, 128 devices: a whole 4x4x4 slice. The times are simulated.
128 devices in a mesh: wide: 32 (over x, z, core), narrow: 4 (over y).
Axes of the slice: x: 4, y: 4, z: 4, core: 2. Of those that a mesh axis runs over, the one named last changes fastest.
Arguments:
- pressure: bfloat16 [16384, 32768], P(None, ('wide', 'narrow')), may hold values from -6 to 6
- weights: float32 [32768], P(('wide', 'narrow')), may hold values from 7.6293945e-06 to 0.00012207031
- green_table: float32 [4, 2, 1024, 32768], P(None, None, None, ('wide', 'narrow')), may hold values from -0.03125 to 0.03125
- starts: int32 [127], replicated, may hold values from 0 to 16128, as said below
- bin_index: int32 [4], replicated, may hold values from 1 to 127, as said below
Outputs:
- mic_power: float32 [1024, 4], P(('wide', 'narrow'))
Inputs may be any that keep to these rules, and one draw needn't show every extreme that they name: Block k starts within 32 samples of k * 128; the first block starts at 0 and the last at 16128. `bin_index`: distinct bins; the lowest is 1 and the highest 256 // 2 - 1.
All inputs are finite; a program needn't handle non-finite values.
Results may differ from a plain program's by a relative error of at most 0.0018.
Values sent between devices are 32-bit elements; how exact they have to be, the bound alone decides.
No kernel may reach another device: no remote copies, remote signals or barrier semaphores. Data moves between devices by JAX's collectives and lax.ppermute only.
A program may use at most 128 MiB of HBM per device.

v0:
```python
import math

import jax
import jax.numpy as jnp
from jax import lax
from jax.sharding import PartitionSpec as P

NFFT = 256
MODES = 4
ITERS = 8


def spectrum_table(bin_index):
    sample = jnp.arange(NFFT, dtype=jnp.int32)
    window = 0.5 - 0.5 * jnp.cos(2.0 * math.pi * sample.astype(jnp.float32) / NFFT)
    norm_scale = 1.0 / jnp.sqrt(jnp.sum(window * window))
    turns = bin_index[:, None] * sample[None, :] % NFFT
    phases = 2.0 * math.pi * turns.astype(jnp.float32) / NFFT
    cos_rows = norm_scale * window[None, :] * jnp.cos(phases)
    sin_rows = -norm_scale * window[None, :] * jnp.sin(phases)
    return jnp.concatenate([cos_rows, sin_rows], 0).astype(jnp.bfloat16)


def block_spectra(pressure, starts, dft_table, nbins):
    offsets = jnp.arange(NFFT, dtype=jnp.int32)
    sample_rows = starts[:, None] + offsets[None, :]
    gathered = jnp.take(pressure, sample_rows, axis=0)
    spectra = jnp.einsum("rt,btp->brp", dft_table, gathered, preferred_element_type=jnp.float32)
    return (spectra[:, :nbins], spectra[:, nbins:])


def gram_of(real_part, imag_part, weights):
    high = lax.Precision.HIGHEST
    wreal = real_part * weights
    wimag = imag_part * weights
    gram_re = jnp.einsum("bfp,cfp->fbc", wreal, real_part, precision=high) + jnp.einsum(
        "bfp,cfp->fbc", wimag, imag_part, precision=high
    )
    gram_im = jnp.einsum("bfp,cfp->fbc", wreal, imag_part, precision=high) - jnp.einsum(
        "bfp,cfp->fbc", wimag, real_part, precision=high
    )
    return jnp.stack([gram_re, gram_im], 0)


def orthonormal(image_re, image_im):
    done_re = []
    done_im = []
    for column in range(image_re.shape[-1]):
        vec_re = image_re[..., column]
        vec_im = image_im[..., column]
        for earlier in range(column):
            prev_re = done_re[earlier]
            prev_im = done_im[earlier]
            coef_re = jnp.sum(prev_re * vec_re + prev_im * vec_im, axis=-1, keepdims=True)
            coef_im = jnp.sum(prev_re * vec_im - prev_im * vec_re, axis=-1, keepdims=True)
            vec_re = vec_re - (coef_re * prev_re - coef_im * prev_im)
            vec_im = vec_im - (coef_re * prev_im + coef_im * prev_re)
        inverse = lax.rsqrt(
            jnp.sum(vec_re * vec_re + vec_im * vec_im, axis=-1, keepdims=True) + 1e-06
        )
        done_re.append(vec_re * inverse)
        done_im.append(vec_im * inverse)
    return (jnp.stack(done_re, -1), jnp.stack(done_im, -1))


def leading_modes(gram):
    high = lax.Precision.HIGHEST
    gram_re = gram[0]
    gram_im = gram[1]
    blocks = gram_re.shape[-1]
    rowpos = jnp.arange(blocks, dtype=jnp.float32) + 0.5
    colpos = jnp.arange(MODES, dtype=jnp.float32) + 1.0
    start_basis = jnp.cos(math.pi * rowpos[:, None] * colpos[None, :] / blocks)
    basis_re = jnp.broadcast_to(start_basis, (gram_re.shape[0], blocks, MODES))
    basis_im = jnp.zeros_like(basis_re)
    for sweep in range(ITERS):
        image_re = jnp.einsum("fbc,fck->fbk", gram_re, basis_re, precision=high) - jnp.einsum(
            "fbc,fck->fbk", gram_im, basis_im, precision=high
        )
        image_im = jnp.einsum("fbc,fck->fbk", gram_re, basis_im, precision=high) + jnp.einsum(
            "fbc,fck->fbk", gram_im, basis_re, precision=high
        )
        basis_re, basis_im = orthonormal(image_re, image_im)
    return (basis_re, basis_im)


def on_device(pressure, weights, green_table, starts, bin_index):
    high = lax.Precision.HIGHEST
    nbins = bin_index.shape[0]
    dft_table = spectrum_table(bin_index)
    real_part, imag_part = block_spectra(pressure, starts, dft_table, nbins)
    green_re = green_table[:, 0]
    green_im = green_table[:, 1]
    proj_re = jnp.einsum("fmp,bfp->mfb", green_re, real_part, precision=high) - jnp.einsum(
        "fmp,bfp->mfb", green_im, imag_part, precision=high
    )
    proj_im = jnp.einsum("fmp,bfp->mfb", green_re, imag_part, precision=high) + jnp.einsum(
        "fmp,bfp->mfb", green_im, real_part, precision=high
    )
    projected = lax.psum_scatter(
        jnp.stack([proj_re, proj_im], 1), ("wide", "narrow"), scatter_dimension=0, tiled=True
    )
    local_gram = gram_of(real_part, imag_part, weights)
    summed_gram = lax.psum(local_gram, ("wide", "narrow"))
    basis_re, basis_im = leading_modes(summed_gram)
    proj_re = projected[:, 0]
    proj_im = projected[:, 1]
    amp_re = jnp.einsum("mfb,fbk->mfk", proj_re, basis_re, precision=high) - jnp.einsum(
        "mfb,fbk->mfk", proj_im, basis_im, precision=high
    )
    amp_im = jnp.einsum("mfb,fbk->mfk", proj_re, basis_im, precision=high) + jnp.einsum(
        "mfb,fbk->mfk", proj_im, basis_re, precision=high
    )
    return jnp.sum(amp_re * amp_re + amp_im * amp_im, axis=-1)


def solution(mesh):
    return jax.shard_map(
        on_device,
        mesh=mesh,
        in_specs=(
            P(None, ("wide", "narrow")),
            P(("wide", "narrow")),
            P(None, None, None, ("wide", "narrow")),
            P(),
            P(),
        ),
        out_specs=P(("wide", "narrow"), None),
        check_vma=False,
    )
```

profile of v0, /device:TPU:1, one launch (start us, length us, event | category | flops | bytes accessed | tf_op | source)
XLA Modules:
  0.0 336.7 jit_solution(5482213357132502622)
XLA Ops:
  6.5 0.6 multiply_reduce_fusion
  7.2 0.7 compare_select_fusion
  7.9 0.8 fusion.45
  9.5 78.0 %gather_fusion = bf16[32512,256]{1,0:T(8,128)(2,1)} fusion(bf16[16384,256]{1,0:T(8,128)(2,1)} %param.5, s32[32768]{0:T(1024)S(1)} %pad_clamp_fusion), kind=kCustom, calls=%fused_computation | custom fusion | bytes 33422336 | tf_op jit(solution)/shard_map/jit(_take)/gather | solution.py:27
  87.6 10.0 %fusion.20 = f32[127,8,256]{2,1,0:T(8,128)S(1)} fusion(bf16[127,256,256]{2,1,0:T(8,128)(2,1)} %bitcast.725, pred[127,256]{1,0:T(8,128)(4,1)S(1)} %fusion.45, bf16[4,256]{1,0:T(4,128)(2,1)S(1)} %get-tuple-element.294, bf16[4,256]{1,0:T(4,128)(2,1)S(1)} %get-tuple-element.293), kind=kOutput, calls=%fused_computation.20 | convolution fusion | flops 141500416 | bytes 17723136 | tf_op jit(solution)/shard_map/rt,btp->brp/dot_general | solution.py:28
  97.7 0.3 broadcast_multiply_fusion
  98.0 0.7 fusion.33
  98.7 0.7 fusion.31
  99.5 4.5 %fusion.6 = f32[4,127,1024]{2,1,0:T(8,128)S(1)} fusion(f32[4,2,1024,256]{3,2,1,0:T(8,128)S(1)} %bitcast.724, f32[127,4,256]{2,1,0:T(4,128)S(1)} %get-tuple-element.291), kind=kOutput, calls=%fused_computation.8 | convolution fusion | flops 1598029824 | bytes 6795264 | tf_op jit(solution)/shard_map/fmp,bfp->mfb/dot_general | solution.py:94
  103.9 4.5 %fusion.4 = f32[4,127,1024]{2,1,0:T(8,128)S(1)} fusion(f32[4,2,1024,256]{3,2,1,0:T(8,128)S(1)} %bitcast.724, f32[127,4,256]{2,1,0:T(4,128)S(1)} %get-tuple-element.292), kind=kOutput, calls=%fused_computation.6 | convolution fusion | flops 1598029824 | bytes 6795264 | tf_op jit(solution)/shard_map/fmp,bfp->mfb/dot_general | solution.py:97
  108.4 0.7 fusion.24
  109.1 0.7 fusion.23
  109.8 4.7 %subtract_bitcast_fusion = f32[1024,1,4,127]{0,3,2,1:T(8,128)S(1)} fusion(f32[4,127,1024]{2,1,0:T(8,128)S(1)} %fusion.6, f32[4,2,1024,256]{3,2,1,0:T(8,128)S(1)} %bitcast.724, f32[127,4,256]{2,1,0:T(4,128)S(1)} %get-tuple-element.292), kind=kOutput, calls=%fused_computation.19 | convolution fusion | flops 1598550016 | bytes 8892416 | tf_op jit(solution)/shard_map/fmp,bfp->mfb/dot_general | solution.py:94
  114.5 4.4 %add_bitcast_fusion = f32[1024,1,4,127]{0,3,2,1:T(8,128)S(1)} fusion(f32[4,127,1024]{2,1,0:T(8,128)S(1)} %fusion.4, f32[4,2,1024,256]{3,2,1,0:T(8,128)S(1)} %bitcast.724, f32[127,4,256]{2,1,0:T(4,128)S(1)} %get-tuple-element.291), kind=kOutput, calls=%fused_computation.18 | convolution fusion | flops 1598550016 | bytes 8892416 | tf_op jit(solution)/shard_map/fmp,bfp->mfb/dot_general | solution.py:97
  119.0 2.3 pad_maximum_fusion
  121.3 5.3 %copy.853 = f32[1024,2,4,127]{3,2,1,0:T(4,128)} copy(f32[1024,2,4,127]{0,3,2,1:T(8,128)} %pad_maximum_fusion) | data formatting | bytes 8323072 | tf_op jit(solution)/shard_map/stack | solution.py:101
  126.6 0.9 pad_maximum_fusion.1
  127.7 158.7 %all-reduce.4.cloned.1.call-done = (f32[1024,2,4,127]{3,2,1,0:T(4,128)}, f32[2,4,127,127]{3,2,1,0:T(8,128)}) async-done(((f32[1024,2,4,127]{3,2,1,0:T(4,128)}, f32[2,4,127,127]{3,2,1,0:T(8,128)}), (f32[1024,2,4,127]{3,2,1,0:T(4,128)}, f32[2,4,127,127]{3,2,1,0:T(8,128)})) %all-reduce.4.cloned.1.call-update) | async-done | bytes 4677680
  286.4 1.5 fusion.77
  287.9 1.5 fusion.61
  289.4 1.5 fusion.76
  290.9 1.5 fusion.60
  292.5 0.3 fusion.220
  293.0 0.2 add_reduce_fusion.44
  293.9 1.5 fusion.75
  295.4 1.5 fusion.58
  297.0 1.5 fusion.59
  298.4 1.5 fusion.74
  300.1 0.3 fusion.206
  301.5 1.5 fusion.73
  302.9 1.5 fusion.56
  304.5 1.5 fusion.57
  306.0 1.5 fusion.72
  307.6 0.3 fusion.192
  309.0 0.5 fusion.71
  309.5 0.5 fusion.54
  310.2 0.5 fusion.55
  310.7 0.5 fusion.70
  311.4 0.3 fusion.178
  311.8 0.2 add_reduce_fusion.26
  312.8 0.5 fusion.69
  313.3 0.5 fusion.52
  313.9 0.5 fusion.53
  314.4 0.5 fusion.68
  315.1 0.3 fusion.164
  315.6 0.2 add_reduce_fusion.20
  316.5 0.5 fusion.67
  317.0 0.5 fusion.50
  317.7 0.5 fusion.51
  318.2 0.5 fusion.66
  318.9 0.3 fusion.150
  320.3 0.5 fusion.65
  320.8 0.5 fusion.48
  321.4 0.5 fusion.49
  321.9 0.5 fusion.64
  322.6 0.3 fusion.136
  323.1 0.2 add_reduce_fusion.8
  324.0 0.5 fusion.63
  324.5 0.5 fusion.46
  325.2 0.5 fusion.47
  325.7 0.5 fusion.62
  326.4 0.3 fusion.122
  327.9 0.7 constant_dynamic-slice_fusion.1
  329.1 0.8 fusion.28
  (147 shorter events, 10.8 us)
Async XLA Ops:
  6.5 279.9 %all-reduce.4.cloned.1.call-start = ((), (), s32[]{:S(2)}) async-start(), calls=%async_computation | async-start | bytes 9437184
  9.5 78.0 %copy-start.2 = (s32[4]{0:T(128)S(1)}, s32[4]{0:T(128)}, u32[]{:S(2)}) copy-start(s32[4]{0:T(128)} %param.9) | copy-start | bytes 52
  87.6 11.8 %slice-start = ((s8[8388608]{0:T(1024)(128)(4,1)}), s8[4194304]{0:T(1024)(128)(4,1)S(1)}, s32[]{:S(2)}) async-start(s8[8388608]{0:T(1024)(128)(4,1)} %bitcast.723), calls=%async_computation.1 | async-start | bytes 8388608
  87.6 10.0 %copy-start.1 = (f32[256]{0:T(256)S(1)}, f32[256]{0:T(256)}, u32[]{:S(2)}) copy-start(f32[256]{0:T(256)} %param.6) | copy-start | bytes 3076
  87.6 11.8 %slice-start.1 = ((s8[8388608]{0:T(1024)(128)(4,1)}), s8[4194304]{0:T(1024)(128)(4,1)S(1)}, s32[]{:S(2)}) async-start(s8[8388608]{0:T(1024)(128)(4,1)} %bitcast.723), calls=%async_computation.2 | async-start | bytes 8388608
  286.4 22.6 %copy-start = (f32[2,4,127,127]{3,2,1,0:T(8,128)S(1)}, f32[2,4,127,127]{3,2,1,0:T(8,128)}, u32[]{:S(2)}) copy-start(f32[2,4,127,127]{3,2,1,0:T(8,128)} %get-tuple-element.118) | copy-start | bytes 1548388
Sparse Core Ops, SparseCore 0:
  127.7 158.6 all-reduce.3
where the time goes:
time: 337 us
  waiting for transfers between devices  159 us (47%)
  local copies, waits for them, and re-layouts  84.1 us (25%)
  matrix products  60.2 us (18%)
  other arithmetic  19 us (6%)
  between operations  14.7 us (4%)
    unnamed x2, waiting for transfers between devices  159 us
    gather x1, local copies, waits for them, and re-layouts, block_spectra(): gathered = jnp.take(pressure, sample_rows, axis=0)  78 us
    dot_general x1, matrix products, block_spectra(): jnp.einsum('rt,btp->brp', dft_table, gathered, preferred_element_type=jnp...  10 us
    dot_general x8, matrix products, leading_modes(): jnp.einsum('fbc,fck->fbk', gram_re, basis_im, precision=high)  7.07 us
    dot_general x8, matrix products, leading_modes(): jnp.einsum('fbc,fck->fbk', gram_im, basis_re, precision=high)  7.07 us
    dot_general x8, matrix products, leading_modes(): jnp.einsum('fbc,fck->fbk', gram_im, basis_im, precision=high)  6.99 us
    dot_general x8, matrix products, leading_modes(): jnp.einsum('fbc,fck->fbk', gram_re, basis_re, precision=high)  6.94 us
  transfers between devices with their start and end apart: 1, of which 1 were waited for; matrix products, arithmetic and copies ran while one was open for 0% of the time, Pallas kernels for 0%

commit v1 on v0

v1 whole, which is shorter than its diff:
```python
import math

import jax
import jax.numpy as jnp
import numpy as np
from jax import lax
from jax.experimental import pallas as pl
from jax.experimental.pallas import tpu as pltpu
from jax.sharding import PartitionSpec as P

NFFT = 256
NB = 127
BINS = 4
MODES = 4
ITERS = 8
MICS = 1024
SAMPLES = 16384
DEVICES = 128
LOCAL = 256
STEP_CHUNKS = 8
STEPS = SAMPLES // (NFFT * STEP_CHUNKS)
AXES = ("wide", "narrow")
NT = (((1,), (1,)), ((), ()))
NN = (((1,), (0,)), ((), ()))
BF = jnp.bfloat16
F32 = jnp.float32


def split(x):
    hi = x.astype(BF)
    return hi, (x - hi.astype(F32)).astype(BF)


def dot(a, b, dims):
    return lax.dot_general(a, b, dims, preferred_element_type=F32)


def gram_kernel(starts_ref, bins_ref, pressure_ref, weights_ref, gram_ref, high_ref, low_ref, table_ref, q_ref):
    step = pl.program_id(0)

    @pl.when(step == 0)
    def _():
        row = lax.broadcasted_iota(jnp.int32, (8, NFFT), 0)
        time = lax.broadcasted_iota(jnp.int32, (8, NFFT), 1)
        which = row & 3
        bins = jnp.where(
            which == 0,
            bins_ref[0],
            jnp.where(which == 1, bins_ref[1], jnp.where(which == 2, bins_ref[2], bins_ref[3])),
        )
        window = 0.5 - 0.5 * jnp.cos(2.0 * math.pi * time.astype(F32) / NFFT)
        scaled = np.float32(1.0 / math.sqrt(0.375 * NFFT)) * window
        phase = 2.0 * math.pi * ((bins * time) & (NFFT - 1)).astype(F32) / NFFT
        rows = jnp.where(row < 4, scaled * jnp.cos(phase), -scaled * jnp.sin(phase))
        table_ref[...] = rows.astype(BF).astype(F32)
        q_ref[...] = jnp.zeros_like(q_ref)

    table = table_ref[...]
    time = lax.broadcasted_iota(jnp.int32, (8, NFFT), 1)
    first = 2 * STEP_CHUNKS * step - 2
    rolled = []
    begins = []
    for k in range(2 * STEP_CHUNKS + 3):
        block = first + k
        start = starts_ref[jnp.clip(block, 0, NB - 1)]
        rolled.append(pltpu.roll(table, start & (NFFT - 1), 1))
        begins.append(jnp.where((block >= 0) & (block < NB), start, 1 << 20))
    for c in range(STEP_CHUNKS):
        base = (step * STEP_CHUNKS + c) * NFFT
        parts = []
        for k in range(5):
            at = time + (base - begins[2 * c + k])
            parts.append(jnp.where((at >= 0) & (at < NFFT), rolled[2 * c + k], 0.0))
        parts.append(jnp.zeros((8, NFFT), F32))
        lhs = jnp.concatenate(parts, 0).astype(BF)
        got = dot(lhs, pressure_ref[c * NFFT : (c + 1) * NFFT, :], NN)
        rows = pl.ds(pl.multiple_of(step * (16 * STEP_CHUNKS) + 16 * c, 8), 40)
        q_ref[0, rows, :] += got[:40, :128]
        q_ref[1, rows, :] += got[:40, 128:]

    @pl.when(step == STEPS - 1)
    def _():
        weights = weights_ref[...]
        upper = lax.broadcasted_iota(jnp.int32, (128, 128), 1) >= lax.broadcasted_iota(jnp.int32, (128, 128), 0)
        for f in range(BINS):
            halves = [
                jnp.concatenate([q_ref[h, pl.ds(16 + g, 128, stride=8), :] for g in (f, 4 + f)], 0)
                for h in range(2)
            ]
            both = jnp.concatenate(halves, 1)
            hi, lo = split(both)
            high_ref[f] = hi
            low_ref[f] = lo
            whi, wlo = split(both * weights)
            prod = dot(whi, hi, NT) + dot(wlo, hi, NT) + dot(whi, lo, NT)
            gram_re = prod[:128, :128] + prod[128:, 128:]
            gram_im = prod[:128, 128:] - prod[128:, :128]
            gram_ref[f * 128 : (f + 1) * 128, :] = jnp.where(upper, gram_re, gram_im)


def local_gram(pressure, weights, starts, bin_index):
    return pl.pallas_call(
        gram_kernel,
        out_shape=(
            jax.ShapeDtypeStruct((BINS * 128, 128), F32),
            jax.ShapeDtypeStruct((BINS, 256, LOCAL), BF),
            jax.ShapeDtypeStruct((BINS, 256, LOCAL), BF),
        ),
        grid_spec=pltpu.PrefetchScalarGridSpec(
            num_scalar_prefetch=2,
            grid=(STEPS,),
            in_specs=[
                pl.BlockSpec((NFFT * STEP_CHUNKS, LOCAL), lambda i, s, b: (i, 0)),
                pl.BlockSpec((1, LOCAL), lambda i, s, b: (0, 0)),
            ],
            out_specs=[
                pl.BlockSpec((BINS * 128, 128), lambda i, s, b: (0, 0)),
                pl.BlockSpec((BINS, 256, LOCAL), lambda i, s, b: (0, 0, 0)),
                pl.BlockSpec((BINS, 256, LOCAL), lambda i, s, b: (0, 0, 0)),
            ],
            scratch_shapes=[pltpu.VMEM((8, NFFT), F32), pltpu.VMEM((2, 1048, 128), F32)],
        ),
        compiler_params=pltpu.CompilerParams(vmem_limit_bytes=24 << 20),
        cost_estimate=pl.CostEstimate(flops=800_000_000, transcendentals=0, bytes_accessed=10_000_000),
        name="gram",
    )(starts, bin_index, pressure, weights.reshape(1, LOCAL))


def project_kernel(left_ref, right_ref, high_ref, low_ref, phigh_ref, plow_ref):
    hi = high_ref[0]
    lo = low_ref[0]
    for tile in range(4):
        cols = slice(tile * 256, (tile + 1) * 256)
        parts = []
        for side in range(2):
            halves = [
                jnp.concatenate([ref[0, side, pl.ds(2 * tile + i, 128, stride=8), :] for i in range(2)], 0)
                for ref in (left_ref, right_ref)
            ]
            mics = jnp.concatenate(halves, 1)
            ghi, glo = split(mics)
            parts.append(dot(hi, ghi, NT) + dot(lo, ghi, NT) + dot(hi, glo, NT))
        by_re, by_im = parts
        phi, plo = split(by_re[:128] - by_im[128:])
        phigh_ref[0, :128, cols] = phi
        plow_ref[0, :128, cols] = plo
        phi, plo = split(by_re[128:] + by_im[:128])
        phigh_ref[0, 128:, cols] = phi
        plow_ref[0, 128:, cols] = plo


def project(green_table, high, low):
    return pl.pallas_call(
        project_kernel,
        out_shape=(
            jax.ShapeDtypeStruct((BINS, 256, MICS), BF),
            jax.ShapeDtypeStruct((BINS, 256, MICS), BF),
        ),
        grid=(BINS,),
        in_specs=[
            pl.BlockSpec((1, 2, MICS, 128), lambda f: (f, 0, 0, 0)),
            pl.BlockSpec((1, 2, MICS, 128), lambda f: (f, 0, 0, 1)),
            pl.BlockSpec((1, 256, LOCAL), lambda f: (f, 0, 0)),
            pl.BlockSpec((1, 256, LOCAL), lambda f: (f, 0, 0)),
        ],
        out_specs=[
            pl.BlockSpec((1, 256, MICS), lambda f: (f, 0, 0)),
            pl.BlockSpec((1, 256, MICS), lambda f: (f, 0, 0)),
        ],
        compiler_params=pltpu.CompilerParams(vmem_limit_bytes=24 << 20),
        cost_estimate=pl.CostEstimate(flops=3_300_000_000, transcendentals=0, bytes_accessed=14_000_000),
        name="project",
    )(green_table, green_table, high, low)


def share_kernel(parts_ref, out_ref):
    total = parts_ref[0:8, :]
    for s in range(1, 64):
        total = total + parts_ref[8 * s : 8 * s + 8, :]
    total = total + pltpu.roll(total, 4, 0)
    for s in range(64):
        out_ref[8 * s : 8 * s + 8, :] = total


def share_sum(parts):
    return pl.pallas_call(
        share_kernel,
        out_shape=jax.ShapeDtypeStruct((512, 128), F32),
        compiler_params=pltpu.CompilerParams(vmem_limit_bytes=4 << 20),
        name="share",
    )(parts)


def modes_kernel(gram_ref, start_ref, phigh_hbm, plow_hbm, out_ref, phigh_ref, plow_ref, sems):
    fetch = [
        pltpu.make_async_copy(phigh_hbm, phigh_ref, sems.at[0]),
        pltpu.make_async_copy(plow_hbm, plow_ref, sems.at[1]),
    ]
    for copy in fetch:
        copy.start()
    col = lax.broadcasted_iota(jnp.int32, (128, 128), 1)
    row = lax.broadcasted_iota(jnp.int32, (128, 128), 0)
    lane_row = lax.broadcasted_iota(jnp.int32, (8, 128), 0)
    sign = jnp.where(lane_row < 4, 1.0, -1.0)
    mats = []
    for f in range(BINS):
        packed = gram_ref[f * 128 : (f + 1) * 128, :]
        flipped = packed.T
        gram_re = jnp.where(col >= row, packed, flipped)
        gram_im = jnp.where(col < row, packed, jnp.where(col > row, -flipped, 0.0))
        mats.append(split(jnp.concatenate([gram_re, gram_im], 1)))
    vecs = [start_ref[...]] * BINS
    for _ in range(ITERS):
        images = []
        for f in range(BINS):
            hi, lo = split(vecs[f])
            ghi, glo = mats[f]
            stacked = jnp.concatenate([hi, lo], 0)
            prod = dot(stacked, ghi, NN)
            prod = prod[:8] + prod[8:] + dot(hi, glo, NN)
            swapped = pltpu.roll(prod[:, 128:], 4, 0)
            images.append(prod[:, :128] + sign * swapped)
        for j in range(MODES):
            for f in range(BINS):
                y = images[f]
                vre = y[j : j + 1, :]
                vim = y[4 + j : 5 + j, :]
                turned = sign * pltpu.roll(y, 4, 0)
                coef = jnp.sum(y * vre + turned * vim, axis=1, keepdims=True)
                inverse = lax.rsqrt(coef[j : j + 1, :] + 1e-06)
                coef = jnp.broadcast_to(coef, (8, 128))
                scaled = coef * (inverse * inverse)
                cross = -sign * pltpu.roll(scaled, 4, 0)
                later = (lane_row & 3) > j
                here = (lane_row & 3) == j
                left = y - (scaled * vre + cross * vim)
                images[f] = jnp.where(later, left, jnp.where(here, y * inverse, y))
        vecs = images
    for copy in fetch:
        copy.wait()
    amps = []
    for f in range(BINS):
        y = vecs[f]
        turned = -sign * pltpu.roll(y, 4, 0)
        hi, lo = split(jnp.concatenate([y, turned], 1))
        prod = dot(jnp.concatenate([hi, lo], 0), phigh_ref[f], NN)
        amps.append(prod[:8] + prod[8:] + dot(hi, plow_ref[f], NN))
    for half in range(2):
        rows = []
        for i in range(4 * half, 4 * half + 4):
            for f in range(BINS):
                rows.append(amps[f][:, i * 128 : (i + 1) * 128])
        out_ref[:, half * 128 : (half + 1) * 128] = jnp.concatenate(rows, 0).T


def start_basis():
    rowpos = np.arange(NB) + 0.5
    colpos = np.arange(MODES) + 1.0
    basis = np.zeros((8, 128), np.float32)
    basis[:MODES, :NB] = np.cos(math.pi * colpos[:, None] * rowpos[None, :] / NB)
    return jnp.asarray(basis)


def amplitudes(gram, phigh, plow):
    return pl.pallas_call(
        modes_kernel,
        out_shape=jax.ShapeDtypeStruct((DEVICES, 256), F32),
        in_specs=[
            pl.BlockSpec((BINS * 128, 128), lambda: (0, 0)),
            pl.BlockSpec((8, 128), lambda: (0, 0)),
            pl.BlockSpec(memory_space=pl.ANY),
            pl.BlockSpec(memory_space=pl.ANY),
        ],
        scratch_shapes=[
            pltpu.VMEM((BINS, 256, MICS), BF),
            pltpu.VMEM((BINS, 256, MICS), BF),
            pltpu.SemaphoreType.DMA((2,)),
        ],
        compiler_params=pltpu.CompilerParams(vmem_limit_bytes=24 << 20),
        name="modes",
    )(gram, start_basis(), phigh, plow)


def power_kernel(parts_ref, out_ref):
    total = jnp.sum(parts_ref[...], axis=0, keepdims=True)
    square = jnp.broadcast_to(total * total, (8, 256))
    lane = lax.broadcasted_iota(jnp.int32, (8, 256), 1)
    mine = (lane >> 5) == lax.broadcasted_iota(jnp.int32, (8, 256), 0)
    cols = []
    for f in range(BINS):
        cols.append(jnp.sum(jnp.where(mine & (((lane >> 3) & 3) == f), square, 0.0), axis=1, keepdims=True))
    out_ref[...] = jnp.concatenate(cols, 1)


def power(parts):
    return pl.pallas_call(
        power_kernel,
        out_shape=jax.ShapeDtypeStruct((MICS // DEVICES, BINS), F32),
        compiler_params=pltpu.CompilerParams(vmem_limit_bytes=4 << 20),
        name="power",
    )(parts)


def exchange(x):
    return lax.all_to_all(x, AXES, 0, 0, tiled=True)


def on_device(pressure, weights, green_table, starts, bin_index):
    gram, high, low = local_gram(pressure, weights, starts, bin_index)
    parts = exchange(gram.reshape(DEVICES, 4, 128))
    phigh, plow = project(green_table, high, low)
    shared = share_sum(parts.reshape(512, 128))
    summed = exchange(shared.reshape(DEVICES, 4, 128)).reshape(512, 128)
    partial = amplitudes(summed, phigh, plow)
    return power(exchange(partial))


def solution(mesh):
    return jax.shard_map(
        on_device,
        mesh=mesh,
        in_specs=(
            P(None, AXES),
            P(AXES),
            P(None, None, None, AXES),
            P(),
            P(),
        ),
        out_specs=P(AXES, None),
        check_vma=False,
    )
```

time: 337 us -> 74.7 us (0.22)
  waiting for transfers between devices: 159 us -> 1.48 us
  local copies, waits for them, and re-layouts: 84.1 us -> 12.5 us
  matrix products: 60.2 us -> 0 us
  blocking collectives: 0 us -> 41 us
  other arithmetic: 19 us -> 0 us
  Pallas kernels: 0 us -> 15.5 us
  between operations: 14.7 us -> 0.07 us
  starting transfers between devices: 0.01 us -> 3.87 us
    unnamed x2 -> x0, waiting for transfers between devices: 159 us -> none
    gather x1 -> x0, local copies, waits for them, and re-layouts: 78 us -> none  [block_spectra(): gathered = jnp.take(pressure, sample_rows, axis=0)]
    dot_general x45 -> x0, matrix products: 60.2 us -> none  [the longest x1 10 us: block_spectra(): jnp.einsum('rt,btp->brp', dft_table, gathered, preferred_element_type=jnp...]
    all_to_all x0 -> x2, blocking collectives: none -> 41 us  [exchange(): return lax.all_to_all(x, AXES, 0, 0, tiled=True)]
    pallas_call x0 -> x5, Pallas kernels: none -> 15.5 us  [the longest x1 5.22 us: amplitudes(): pl.pallas_call(modes_kernel, out_shape=jax.ShapeDtypeStruct((DEVICES, 256...]
    unnamed x10 -> x17, local copies, waits for them, and re-layouts: 0.03 us -> 11.7 us
    reduce_sum x57 -> x0, other arithmetic: 11.6 us -> none  [the longest x32 5.51 us: orthonormal(): jnp.sum(vec_re * vec_re + vec_im * vec_im, axis=-1, keepdims=True) + 1e-06]
    another operation x1 -> x0, local copies, waits for them, and re-layouts: 5.34 us -> none  [on_device(): jnp.stack([proj_re, proj_im], 1)]
  transfers between devices with their start and end apart: 1 -> 1, of which waited for: 1 -> 1; matrix products, arithmetic and copies ran while one was open for 0% -> 0% of each run, Pallas kernels for 0% -> 7%
where the time goes in v1:
time: 74.7 us; the launch traced here: 74.4 us
  blocking collectives  41 us (55%)
  Pallas kernels  15.5 us (21%)
  local copies, waits for them, and re-layouts  12.5 us (17%)
  starting transfers between devices  3.87 us (5%)
  waiting for transfers between devices  1.48 us (2%)
    all_to_all x2, blocking collectives, exchange(): return lax.all_to_all(x, AXES, 0, 0, tiled=True)  41 us
    unnamed x17, local copies, waits for them, and re-layouts  11.7 us
    pallas_call x1, Pallas kernels, amplitudes(): pl.pallas_call(modes_kernel, out_shape=jax.ShapeDtypeStruct((DEVICES, 256...  5.22 us
    pallas_call x1, Pallas kernels, project(): pl.pallas_call(project_kernel, out_shape=(jax.ShapeDtypeStruct((BINS, 256...  5.12 us
    pallas_call x1, Pallas kernels, local_gram(): pl.pallas_call(gram_kernel, out_shape=(jax.ShapeDtypeStruct((BINS * 128,...  4.24 us
    all_to_all x1, starting transfers between devices, exchange(): return lax.all_to_all(x, AXES, 0, 0, tiled=True)  3.87 us
  transfers between devices with their start and end apart: 1, of which 1 were waited for; matrix products, arithmetic and copies ran while one was open for 0% of the time, Pallas kernels for 7%

profile of v1, /device:TPU:1, one launch (start us, length us, event | category | flops | bytes accessed | tf_op | source)
XLA Modules:
  0.0 74.4 jit_solution(12306177267175200284)
XLA Ops:
  0.0 0.0 copy-start.1
  0.0 3.4 %copy-done.1 = bf16[16384,256]{1,0:T(8,128)(2,1)S(1)} copy-done((bf16[16384,256]{1,0:T(8,128)(2,1)S(1)}, bf16[16384,256]{1,0:T(8,128)(2,1)}, u32[]{:S(2)}) %copy-start.1) | copy-done | bytes 8388632
  3.4 0.0 copy-start.5
  3.4 0.7 copy-done.5
  4.1 0.0 copy-start.6
  4.1 0.7 copy-done.6
  4.7 0.0 copy-start.7
  4.7 0.7 copy-done.7
  5.4 4.2 %gram.1 = (f32[512,128]{1,0:T(8,128)S(1)}, bf16[4,256,256]{2,1,0:T(8,128)(2,1)S(1)}, bf16[4,256,256]{2,1,0:T(8,128)(2,1)S(1)}) custom-call(s32[127]{0:T(128)S(1)} %copy-done.6, s32[4]{0:T(128)S(1)} %copy-done.7, bf16[16384,256]{1,0:T(8,128)(2,1)S(1)} %copy-done.1, f32[1,256]{1,0:T(1,128)S(1)} %bitcast.14), custom_call_target="tpu_custom_call" | custom-call | flops 800000000 | bytes 10000000 | tf_op jit(solution)/shard_map/gram/pallas_call | solution.py:102
  9.6 22.6 %all_to_all.21 = f32[128,4,128]{2,1,0:T(4,128)S(1)} all-to-all(f32[128,4,128]{2,1,0:T(4,128)S(1)} %bitcast.13), channel_id=1, replica_groups=mesh['wide'=32,'narrow'=4] {'wide','narrow'}, dimensions={0} | all-to-all | bytes 524288 | tf_op jit(solution)/shard_map/all_to_all | solution.py:305
  32.3 0.8 %share.1 = f32[512,128]{1,0:T(8,128)} custom-call(f32[512,128]{1,0:T(8,128)S(1)} %bitcast.9), custom_call_target="tpu_custom_call" | custom-call | tf_op jit(solution)/shard_map/share/pallas_call | solution.py:186
  33.0 3.9 %all-to-all-start.1 = ((f32[128,4,128]{2,1,0:T(4,128)}), f32[128,4,128]{2,1,0:T(4,128)S(1)}, u32[]{:S(2)}, u32[]{:S(2)}) async-start(f32[128,4,128]{2,1,0:T(4,128)} %bitcast.3), calls=%async_computation.1 | async-start | bytes 524288 | tf_op jit(solution)/shard_map/all_to_all | solution.py:305
  36.9 0.0 copy-start
  36.9 3.4 %copy-done = f32[4,2,1024,256]{3,2,1,0:T(8,128)S(1)} copy-done((f32[4,2,1024,256]{3,2,1,0:T(8,128)S(1)}, f32[4,2,1024,256]{3,2,1,0:T(8,128)}, u32[]{:S(2)}) %copy-start) | copy-done | bytes 8388632
  40.3 0.0 copy-start.4
  40.3 5.1 %project.1 = (bf16[4,256,1024]{2,1,0:T(8,128)(2,1)S(1)}, bf16[4,256,1024]{2,1,0:T(8,128)(2,1)S(1)}) custom-call(f32[4,2,1024,256]{3,2,1,0:T(8,128)S(1)} %copy-done, f32[4,2,1024,256]{3,2,1,0:T(8,128)S(1)} %copy-done, bf16[4,256,256]{2,1,0:T(8,128)(2,1)S(1)} %get-tuple-element.11.high_ref, bf16[4,256,256]{2,1,0:T(8,128)(2,1)S(1)} %get-tuple-element.12.low_ref), custom_call_target="tpu_custom_call" | custom-call | flops 3300000000 | bytes 14000000 | tf_op jit(solution)/shard_map/project/pallas_call | solution.py:153
  45.4 0.0 copy-start.2
  45.4 1.3 %copy-done.2 = bf16[4,256,1024]{2,1,0:T(8,128)(2,1)} copy-done((bf16[4,256,1024]{2,1,0:T(8,128)(2,1)}, bf16[4,256,1024]{2,1,0:T(8,128)(2,1)S(1)}, u32[]{:S(2)}) %copy-start.2) | copy-done | bytes 2097176
  46.8 1.5 %all-to-all-done.1 = f32[128,4,128]{2,1,0:T(4,128)S(1)} async-done(((f32[128,4,128]{2,1,0:T(4,128)}), f32[128,4,128]{2,1,0:T(4,128)S(1)}, u32[]{:S(2)}, u32[]{:S(2)}) %all-to-all-start.1) | async-done | bytes 262176 | tf_op jit(solution)/shard_map/all_to_all | solution.py:305
  48.2 0.0 copy-done.4
  48.2 0.0 copy-start.3
  48.2 1.6 %copy-done.3 = bf16[4,256,1024]{2,1,0:T(8,128)(2,1)S(1)} copy-done((bf16[4,256,1024]{2,1,0:T(8,128)(2,1)S(1)}, bf16[4,256,1024]{2,1,0:T(8,128)(2,1)}, u32[]{:S(2)}) %copy-start.3) | copy-done | bytes 2097176
  49.8 5.2 %modes.1 = f32[128,256]{1,0:T(8,128)S(1)} custom-call(f32[512,128]{1,0:T(8,128)S(1)} %bitcast.10, f32[8,128]{1,0:T(8,128)S(1)} %copy-done.4, bf16[4,256,1024]{2,1,0:T(8,128)(2,1)S(1)} %get-tuple-element.13.phigh_hbm, bf16[4,256,1024]{2,1,0:T(8,128)(2,1)S(1)} %copy-done.3), custom_call_target="tpu_custom_call" | custom-call | tf_op jit(solution)/shard_map/modes/pallas_call | solution.py:265
  55.1 0.1 copy.8
  55.2 18.4 %all_to_all.22 = f32[128,1,256]{2,1,0:T(1,128)S(1)} all-to-all(f32[128,1,256]{2,1,0:T(1,128)S(1)} %copy.8), channel_id=1, replica_groups=mesh['wide'=32,'narrow'=4] {'wide','narrow'}, dimensions={0} | all-to-all | bytes 262144 | tf_op jit(solution)/shard_map/all_to_all | solution.py:305
  73.6 0.1 power.1
  73.7 0.7 copy.9
  (1 shorter events, 0.0 us)
Async XLA Ops:
  0.0 3.4 %copy-start.1 = (bf16[16384,256]{1,0:T(8,128)(2,1)S(1)}, bf16[16384,256]{1,0:T(8,128)(2,1)}, u32[]{:S(2)}) copy-start(bf16[16384,256]{1,0:T(8,128)(2,1)} %pressure_ref.1) | copy-start | bytes 25165828
  3.4 0.7 copy-start.5
  4.1 0.7 copy-start.6
  4.7 0.7 copy-start.7
  33.0 15.2 %all-to-all-start.1 = ((f32[128,4,128]{2,1,0:T(4,128)}), f32[128,4,128]{2,1,0:T(4,128)S(1)}, u32[]{:S(2)}, u32[]{:S(2)}) async-start(f32[128,4,128]{2,1,0:T(4,128)} %bitcast.3), calls=%async_computation.1 | async-start | bytes 524288 | tf_op jit(solution)/shard_map/all_to_all | solution.py:305
  36.9 3.4 %copy-start = (f32[4,2,1024,256]{3,2,1,0:T(8,128)S(1)}, f32[4,2,1024,256]{3,2,1,0:T(8,128)}, u32[]{:S(2)}) copy-start(f32[4,2,1024,256]{3,2,1,0:T(8,128)} %right_ref.1) | copy-start | bytes 25165828
  40.3 7.9 %copy-start.4 = (f32[8,128]{1,0:T(8,128)S(1)}, f32[8,128]{1,0:T(8,128)}, u32[]{:S(2)}) copy-start(f32[8,128]{1,0:T(8,128)} %constant.2.clone.start_ref) | copy-start | bytes 12292
  45.4 1.3 %copy-start.2 = (bf16[4,256,1024]{2,1,0:T(8,128)(2,1)}, bf16[4,256,1024]{2,1,0:T(8,128)(2,1)S(1)}, u32[]{:S(2)}) copy-start(bf16[4,256,1024]{2,1,0:T(8,128)(2,1)S(1)} %get-tuple-element.14.plow_hbm) | copy-start | bytes 6291460
  48.2 1.6 %copy-start.3 = (bf16[4,256,1024]{2,1,0:T(8,128)(2,1)S(1)}, bf16[4,256,1024]{2,1,0:T(8,128)(2,1)}, u32[]{:S(2)}) copy-start(bf16[4,256,1024]{2,1,0:T(8,128)(2,1)} %copy-done.2) | copy-start | bytes 6291460

commit v2 on v1

--- a/solution.py
+++ b/solution.py
@@ -18,7 +18,8 @@
 DEVICES = 128
 LOCAL = 256
 STEP_CHUNKS = 8
-STEPS = SAMPLES // (NFFT * STEP_CHUNKS)
+STEP_ROWS = NFFT * STEP_CHUNKS
+STEPS = SAMPLES // STEP_ROWS
 AXES = ("wide", "narrow")
 NT = (((1,), (1,)), ((), ()))
 NN = (((1,), (0,)), ((), ()))
@@ -35,70 +36,92 @@
     return lax.dot_general(a, b, dims, preferred_element_type=F32)
 
 
-def gram_kernel(starts_ref, bins_ref, pressure_ref, weights_ref, gram_ref, high_ref, low_ref, table_ref, q_ref):
-    step = pl.program_id(0)
-
-    @pl.when(step == 0)
-    def _():
-        row = lax.broadcasted_iota(jnp.int32, (8, NFFT), 0)
-        time = lax.broadcasted_iota(jnp.int32, (8, NFFT), 1)
-        which = row & 3
-        bins = jnp.where(
-            which == 0,
-            bins_ref[0],
-            jnp.where(which == 1, bins_ref[1], jnp.where(which == 2, bins_ref[2], bins_ref[3])),
-        )
-        window = 0.5 - 0.5 * jnp.cos(2.0 * math.pi * time.astype(F32) / NFFT)
-        scaled = np.float32(1.0 / math.sqrt(0.375 * NFFT)) * window
-        phase = 2.0 * math.pi * ((bins * time) & (NFFT - 1)).astype(F32) / NFFT
-        rows = jnp.where(row < 4, scaled * jnp.cos(phase), -scaled * jnp.sin(phase))
-        table_ref[...] = rows.astype(BF).astype(F32)
-        q_ref[...] = jnp.zeros_like(q_ref)
-
-    table = table_ref[...]
+def gram_kernel(
+    starts_hbm, bins_hbm, weights_hbm, pressure_hbm, gram_ref, high_ref, low_ref,
+    starts_ref, bins_ref, weights_ref, pressure_ref, q_ref, small_sems, sems,
+):
+    small = [
+        pltpu.make_async_copy(starts_hbm, starts_ref, small_sems.at[0]),
+        pltpu.make_async_copy(bins_hbm, bins_ref, small_sems.at[1]),
+        pltpu.make_async_copy(weights_hbm, weights_ref, small_sems.at[2]),
+    ]
+
+    def chunk_copy(step):
+        rows = pl.ds(pl.multiple_of(step * STEP_ROWS, STEP_ROWS), STEP_ROWS)
+        return pltpu.make_async_copy(pressure_hbm.at[rows, :], pressure_ref.at[rows, :], sems.at[step])
+
+    for copy in small:
+        copy.start()
+    for step in range(STEPS):
+        chunk_copy(step).start()
+
+    q_ref[...] = jnp.zeros_like(q_ref)
+    row = lax.broadcasted_iota(jnp.int32, (8, NFFT), 0)
     time = lax.broadcasted_iota(jnp.int32, (8, NFFT), 1)
-    first = 2 * STEP_CHUNKS * step - 2
-    rolled = []
-    begins = []
-    for k in range(2 * STEP_CHUNKS + 3):
-        block = first + k
-        start = starts_ref[jnp.clip(block, 0, NB - 1)]
-        rolled.append(pltpu.roll(table, start & (NFFT - 1), 1))
-        begins.append(jnp.where((block >= 0) & (block < NB), start, 1 << 20))
-    for c in range(STEP_CHUNKS):
-        base = (step * STEP_CHUNKS + c) * NFFT
-        parts = []
-        for k in range(5):
-            at = time + (base - begins[2 * c + k])
-            parts.append(jnp.where((at >= 0) & (at < NFFT), rolled[2 * c + k], 0.0))
-        parts.append(jnp.zeros((8, NFFT), F32))
-        lhs = jnp.concatenate(parts, 0).astype(BF)
-        got = dot(lhs, pressure_ref[c * NFFT : (c + 1) * NFFT, :], NN)
-        rows = pl.ds(pl.multiple_of(step * (16 * STEP_CHUNKS) + 16 * c, 8), 40)
-        q_ref[0, rows, :] += got[:40, :128]
-        q_ref[1, rows, :] += got[:40, 128:]
-
-    @pl.when(step == STEPS - 1)
-    def _():
-        weights = weights_ref[...]
-        upper = lax.broadcasted_iota(jnp.int32, (128, 128), 1) >= lax.broadcasted_iota(jnp.int32, (128, 128), 0)
-        for f in range(BINS):
-            halves = [
-                jnp.concatenate([q_ref[h, pl.ds(16 + g, 128, stride=8), :] for g in (f, 4 + f)], 0)
-                for h in range(2)
-            ]
-            both = jnp.concatenate(halves, 1)
-            hi, lo = split(both)
-            high_ref[f] = hi
-            low_ref[f] = lo
-            whi, wlo = split(both * weights)
-            prod = dot(whi, hi, NT) + dot(wlo, hi, NT) + dot(whi, lo, NT)
-            gram_re = prod[:128, :128] + prod[128:, 128:]
-            gram_im = prod[:128, 128:] - prod[128:, :128]
-            gram_ref[f * 128 : (f + 1) * 128, :] = jnp.where(upper, gram_re, gram_im)
+    which = row & 3
+    window = 0.5 - 0.5 * jnp.cos(2.0 * math.pi * time.astype(F32) / NFFT)
+    scaled = np.float32(1.0 / math.sqrt(0.375 * NFFT)) * window
+    for copy in small:
+        copy.wait()
+    bins = jnp.where(
+        which == 0,
+        bins_ref[0],
+        jnp.where(which == 1, bins_ref[1], jnp.where(which == 2, bins_ref[2], bins_ref[3])),
+    )
+    phase = 2.0 * math.pi * ((bins * time) & (NFFT - 1)).astype(F32) / NFFT
+    table = jnp.where(row < 4, scaled * jnp.cos(phase), -scaled * jnp.sin(phase))
+    table = table.astype(BF).astype(F32)
+
+    def one_step(step, carry):
+        first = 2 * STEP_CHUNKS * step - 2
+        rolled = []
+        begins = []
+        for k in range(2 * STEP_CHUNKS + 3):
+            block = first + k
+            start = starts_ref[jnp.clip(block, 0, NB - 1)]
+            rolled.append(pltpu.roll(table, start & (NFFT - 1), 1))
+            begins.append(jnp.where((block >= 0) & (block < NB), start, 1 << 20))
+        chunk_copy(step).wait()
+        for c in range(STEP_CHUNKS):
+            base = (step * STEP_CHUNKS + c) * NFFT
+            parts = []
+            for k in range(5):
+                at = time + (base - begins[2 * c + k])
+                parts.append(jnp.where((at >= 0) & (at < NFFT), rolled[2 * c + k], 0.0))
+            parts.append(jnp.zeros((8, NFFT), F32))
+            lhs = jnp.concatenate(parts, 0).astype(BF)
+            rows = pl.ds(pl.multiple_of(base, NFFT), NFFT)
+            got = dot(lhs, pressure_ref[rows, :], NN)
+            rows = pl.ds(pl.multiple_of(step * (16 * STEP_CHUNKS) + 16 * c, 8), 40)
+            q_ref[0, rows, :] += got[:40, :128]
+            q_ref[1, rows, :] += got[:40, 128:]
+        return carry
+
+    lax.fori_loop(0, STEPS, one_step, 0)
+
+    weights = weights_ref[...]
+    upper = lax.broadcasted_iota(jnp.int32, (128, 128), 1) >= lax.broadcasted_iota(jnp.int32, (128, 128), 0)
+    for f in range(BINS):
+        halves = [
+            jnp.concatenate([q_ref[h, pl.ds(16 + g, 128, stride=8), :] for g in (f, 4 + f)], 0) for h in range(2)
+        ]
+        both = jnp.concatenate(halves, 1)
+        hi, lo = split(both)
+        high_ref[f] = hi
+        low_ref[f] = lo
+        whi, wlo = split(both * weights)
+        prod = dot(whi, hi, NT) + dot(wlo, hi, NT) + dot(whi, lo, NT)
+        gram_re = prod[:128, :128] + prod[128:, 128:]
+        gram_im = prod[:128, 128:] - prod[128:, :128]
+        gram_ref[f * 128 : (f + 1) * 128, :] = jnp.where(upper, gram_re, gram_im)
+
+
+def in_hbm(x):
+    return pltpu.with_memory_space_constraint(x, pltpu.HBM)
 
 
 def local_gram(pressure, weights, starts, bin_index):
+    hbm = pl.BlockSpec(memory_space=pltpu.HBM)
     return pl.pallas_call(
         gram_kernel,
         out_shape=(
@@ -106,24 +129,20 @@
             jax.ShapeDtypeStruct((BINS, 256, LOCAL), BF),
             jax.ShapeDtypeStruct((BINS, 256, LOCAL), BF),
         ),
-        grid_spec=pltpu.PrefetchScalarGridSpec(
-            num_scalar_prefetch=2,
-            grid=(STEPS,),
-            in_specs=[
-                pl.BlockSpec((NFFT * STEP_CHUNKS, LOCAL), lambda i, s, b: (i, 0)),
-                pl.BlockSpec((1, LOCAL), lambda i, s, b: (0, 0)),
-            ],
-            out_specs=[
-                pl.BlockSpec((BINS * 128, 128), lambda i, s, b: (0, 0)),
-                pl.BlockSpec((BINS, 256, LOCAL), lambda i, s, b: (0, 0, 0)),
-                pl.BlockSpec((BINS, 256, LOCAL), lambda i, s, b: (0, 0, 0)),
-            ],
-            scratch_shapes=[pltpu.VMEM((8, NFFT), F32), pltpu.VMEM((2, 1048, 128), F32)],
-        ),
+        in_specs=[hbm] * 4,
+        scratch_shapes=[
+            pltpu.SMEM((NB,), jnp.int32),
+            pltpu.SMEM((BINS,), jnp.int32),
+            pltpu.VMEM((1, LOCAL), F32),
+            pltpu.VMEM((SAMPLES, LOCAL), BF),
+            pltpu.VMEM((2, 1048, 128), F32),
+            pltpu.SemaphoreType.DMA((3,)),
+            pltpu.SemaphoreType.DMA((STEPS,)),
+        ],
         compiler_params=pltpu.CompilerParams(vmem_limit_bytes=24 << 20),
         cost_estimate=pl.CostEstimate(flops=800_000_000, transcendentals=0, bytes_accessed=10_000_000),
         name="gram",
-    )(starts, bin_index, pressure, weights.reshape(1, LOCAL))
+    )(in_hbm(starts), in_hbm(bin_index), in_hbm(weights.reshape(1, LOCAL)), in_hbm(pressure))
 
 
 def project_kernel(left_ref, right_ref, high_ref, low_ref, phigh_ref, plow_ref):
@@ -153,8 +172,8 @@
     return pl.pallas_call(
         project_kernel,
         out_shape=(
-            jax.ShapeDtypeStruct((BINS, 256, MICS), BF),
-            jax.ShapeDtypeStruct((BINS, 256, MICS), BF),
+            pltpu.HBM((BINS, 256, MICS), BF),
+            pltpu.HBM((BINS, 256, MICS), BF),
         ),
         grid=(BINS,),
         in_specs=[
@@ -170,7 +189,7 @@
         compiler_params=pltpu.CompilerParams(vmem_limit_bytes=24 << 20),
         cost_estimate=pl.CostEstimate(flops=3_300_000_000, transcendentals=0, bytes_accessed=14_000_000),
         name="project",
-    )(green_table, green_table, high, low)
+    )(in_hbm(green_table), in_hbm(green_table), high, low)
 
 
 def share_kernel(parts_ref, out_ref):
@@ -250,7 +269,7 @@
         for i in range(4 * half, 4 * half + 4):
             for f in range(BINS):
                 rows.append(amps[f][:, i * 128 : (i + 1) * 128])
-        out_ref[:, half * 128 : (half + 1) * 128] = jnp.concatenate(rows, 0).T
+        out_ref[pl.ds(half, 128, stride=2), :] = jnp.concatenate(rows, 0).T
 
 
 def start_basis():
@@ -264,13 +283,8 @@
 def amplitudes(gram, phigh, plow):
     return pl.pallas_call(
         modes_kernel,
-        out_shape=jax.ShapeDtypeStruct((DEVICES, 256), F32),
-        in_specs=[
-            pl.BlockSpec((BINS * 128, 128), lambda: (0, 0)),
-            pl.BlockSpec((8, 128), lambda: (0, 0)),
-            pl.BlockSpec(memory_space=pl.ANY),
-            pl.BlockSpec(memory_space=pl.ANY),
-        ],
+        out_shape=jax.ShapeDtypeStruct((2 * DEVICES, 128), F32),
+        in_specs=[pl.BlockSpec(memory_space=pltpu.VMEM)] * 2 + [pl.BlockSpec(memory_space=pltpu.HBM)] * 2,
         scratch_shapes=[
             pltpu.VMEM((BINS, 256, MICS), BF),
             pltpu.VMEM((BINS, 256, MICS), BF),
@@ -278,27 +292,35 @@
         ],
         compiler_params=pltpu.CompilerParams(vmem_limit_bytes=24 << 20),
         name="modes",
-    )(gram, start_basis(), phigh, plow)
+    )(gram, start_basis(), in_hbm(phigh), in_hbm(plow))
 
 
 def power_kernel(parts_ref, out_ref):
-    total = jnp.sum(parts_ref[...], axis=0, keepdims=True)
-    square = jnp.broadcast_to(total * total, (8, 256))
-    lane = lax.broadcasted_iota(jnp.int32, (8, 256), 1)
-    mine = (lane >> 5) == lax.broadcasted_iota(jnp.int32, (8, 256), 0)
-    cols = []
-    for f in range(BINS):
-        cols.append(jnp.sum(jnp.where(mine & (((lane >> 3) & 3) == f), square, 0.0), axis=1, keepdims=True))
-    out_ref[...] = jnp.concatenate(cols, 1)
+    total = parts_ref[0:8, :]
+    for s in range(1, 32):
+        total = total + parts_ref[8 * s : 8 * s + 8, :]
+    total = total + pltpu.roll(total, 4, 0)
+    total = total + pltpu.roll(total, 6, 0)
+    square = total * total
+    lane = lax.broadcasted_iota(jnp.int32, (8, 128), 1)
+    row = lax.broadcasted_iota(jnp.int32, (8, 128), 0)
+    mic = lax.broadcasted_iota(jnp.int32, (8, 8), 1)
+    out = jnp.zeros((8, 8), F32)
+    for half in range(2):
+        source = jnp.broadcast_to(square[half : half + 1, :], (8, 128))
+        for i in range(4):
+            sums = jnp.sum(jnp.where((lane >> 3) == 4 * i + row, source, 0.0), axis=1, keepdims=True)
+            out = jnp.where(mic == 4 * half + i, sums, out)
+    out_ref[...] = out[:BINS, :]
 
 
 def power(parts):
     return pl.pallas_call(
         power_kernel,
-        out_shape=jax.ShapeDtypeStruct((MICS // DEVICES, BINS), F32),
+        out_shape=jax.ShapeDtypeStruct((BINS, MICS // DEVICES), F32),
         compiler_params=pltpu.CompilerParams(vmem_limit_bytes=4 << 20),
         name="power",
-    )(parts)
+    )(parts).T
 
 
 def exchange(x):
@@ -312,7 +334,7 @@
     shared = share_sum(parts.reshape(512, 128))
     summed = exchange(shared.reshape(DEVICES, 4, 128)).reshape(512, 128)
     partial = amplitudes(summed, phigh, plow)
-    return power(exchange(partial))
+    return power(exchange(partial.reshape(DEVICES, 2, 128)).reshape(2 * DEVICES, 128))
 
 
 def solution(mesh):

time: 74.7 us -> 68.3 us (0.914)
  local copies, waits for them, and re-layouts: 12.5 us -> 0.01 us
  Pallas kernels: 15.5 us -> 21.7 us
  blocking collectives: 41 us -> 39.2 us
  waiting for transfers between devices: 1.48 us -> 3.27 us
    unnamed x17 -> x2, local copies, waits for them, and re-layouts: 11.7 us -> 0.01 us
    pallas_call x3, Pallas kernels: 10.4 us -> 13.7 us  [the longest x1 8.04 us: project(): pl.pallas_call(project_kernel, out_shape=(pltpu.HBM((BINS, 256, MICS), BF...]
    pallas_call x1, Pallas kernels: 4.24 us -> 7.25 us  [local_gram(): pl.pallas_call(gram_kernel, out_shape=(jax.ShapeDtypeStruct((BINS * 128,...]
    all_to_all x2, blocking collectives: 41 us -> 39.2 us  [exchange(): return lax.all_to_all(x, AXES, 0, 0, tiled=True)]
    all_to_all x1, waiting for transfers between devices: 1.48 us -> 3.27 us  [exchange(): return lax.all_to_all(x, AXES, 0, 0, tiled=True)]
  transfers between devices with their start and end apart: 1 -> 1, of which waited for: 1 -> 1; matrix products, arithmetic and copies ran while one was open for 0% -> 0% of each run, Pallas kernels for 7% -> 12%
where the time goes in v2:
time: 68.3 us; the launch traced here: 68.1 us
  blocking collectives  39.2 us (57%)
  Pallas kernels  21.7 us (32%)
  starting transfers between devices  3.87 us (6%)
  waiting for transfers between devices  3.27 us (5%)
    all_to_all x2, blocking collectives, exchange(): return lax.all_to_all(x, AXES, 0, 0, tiled=True)  39.2 us
    pallas_call x1, Pallas kernels, project(): pl.pallas_call(project_kernel, out_shape=(pltpu.HBM((BINS, 256, MICS), BF...  8.04 us
    pallas_call x1, Pallas kernels, local_gram(): pl.pallas_call(gram_kernel, out_shape=(jax.ShapeDtypeStruct((BINS * 128,...  7.25 us
    pallas_call x1, Pallas kernels, amplitudes(): pl.pallas_call(modes_kernel, out_shape=jax.ShapeDtypeStruct((2 * DEVICES,...  4.95 us
    all_to_all x1, starting transfers between devices, exchange(): return lax.all_to_all(x, AXES, 0, 0, tiled=True)  3.87 us
    all_to_all x1, waiting for transfers between devices, exchange(): return lax.all_to_all(x, AXES, 0, 0, tiled=True)  3.27 us
  transfers between devices with their start and end apart: 1, of which 1 were waited for; matrix products, arithmetic and copies ran while one was open for 0% of the time, Pallas kernels for 12%

profile of v2, /device:TPU:1, one launch (start us, length us, event | category | flops | bytes accessed | tf_op | source)
XLA Modules:
  0.0 68.1 jit_solution(138943548740044992)
XLA Ops:
  0.0 7.2 %gram.1 = (f32[512,128]{1,0:T(8,128)S(1)}, bf16[4,256,256]{2,1,0:T(8,128)(2,1)S(1)}, bf16[4,256,256]{2,1,0:T(8,128)(2,1)S(1)}) custom-call(s32[127]{0:T(128)} %starts_hbm.1, s32[4]{0:T(128)} %bins_hbm.1, f32[1,256]{1,0:T(1,128)} %bitcast.13, bf16[16384,256]{1,0:T(8,128)(2,1)} %pressure_hbm.1), custom_call_target="tpu_custom_call" | custom-call | flops 800000000 | bytes 10000000 | tf_op jit(solution)/shard_map/gram/pallas_call | solution.py:125
  7.3 22.6 %all_to_all.15 = f32[128,4,128]{2,1,0:T(4,128)S(1)} all-to-all(f32[128,4,128]{2,1,0:T(4,128)S(1)} %bitcast.12), channel_id=1, replica_groups=mesh['wide'=32,'narrow'=4] {'wide','narrow'}, dimensions={0} | all-to-all | bytes 524288 | tf_op jit(solution)/shard_map/all_to_all | solution.py:327
  29.9 0.8 %share.1 = f32[512,128]{1,0:T(8,128)} custom-call(f32[512,128]{1,0:T(8,128)S(1)} %bitcast.8), custom_call_target="tpu_custom_call" | custom-call | tf_op jit(solution)/shard_map/share/pallas_call | solution.py:205
  30.7 3.9 %all-to-all-start.1 = ((f32[128,4,128]{2,1,0:T(4,128)}), f32[128,4,128]{2,1,0:T(4,128)S(1)}, u32[]{:S(2)}, u32[]{:S(2)}) async-start(f32[128,4,128]{2,1,0:T(4,128)} %bitcast.3), calls=%async_computation.1 | async-start | bytes 524288 | tf_op jit(solution)/shard_map/all_to_all | solution.py:327
  34.5 0.0 copy-start
  34.6 8.0 %project.1 = (bf16[4,256,1024]{2,1,0:T(8,128)(2,1)}, bf16[4,256,1024]{2,1,0:T(8,128)(2,1)}) custom-call(f32[4,2,1024,256]{3,2,1,0:T(8,128)} %right_ref.1, f32[4,2,1024,256]{3,2,1,0:T(8,128)} %right_ref.1, bf16[4,256,256]{2,1,0:T(8,128)(2,1)S(1)} %get-tuple-element.11.high_ref, bf16[4,256,256]{2,1,0:T(8,128)(2,1)S(1)} %get-tuple-element.12.low_ref), custom_call_target="tpu_custom_call" | custom-call | flops 3300000000 | bytes 14000000 | tf_op jit(solution)/shard_map/project/pallas_call | solution.py:172
  42.6 3.3 %all-to-all-done.1 = f32[128,4,128]{2,1,0:T(4,128)S(1)} async-done(((f32[128,4,128]{2,1,0:T(4,128)}), f32[128,4,128]{2,1,0:T(4,128)S(1)}, u32[]{:S(2)}, u32[]{:S(2)}) %all-to-all-start.1) | async-done | bytes 262176 | tf_op jit(solution)/shard_map/all_to_all | solution.py:327
  45.9 0.0 copy-done
  45.9 4.9 %modes.1 = f32[256,128]{1,0:T(8,128)S(1)} custom-call(f32[512,128]{1,0:T(8,128)S(1)} %bitcast.9, f32[8,128]{1,0:T(8,128)S(1)} %copy-done, bf16[4,256,1024]{2,1,0:T(8,128)(2,1)} %get-tuple-element.13.phigh_hbm, bf16[4,256,1024]{2,1,0:T(8,128)(2,1)} %get-tuple-element.14.plow_hbm), custom_call_target="tpu_custom_call" | custom-call | tf_op jit(solution)/shard_map/modes/pallas_call | solution.py:284
  50.8 16.5 %all_to_all.16 = f32[128,2,128]{2,1,0:T(2,128)S(1)} all-to-all(f32[128,2,128]{2,1,0:T(2,128)S(1)} %bitcast.11), channel_id=1, replica_groups=mesh['wide'=32,'narrow'=4] {'wide','narrow'}, dimensions={0} | all-to-all | bytes 262144 | tf_op jit(solution)/shard_map/all_to_all | solution.py:327
  67.4 0.7 %power.1 = f32[4,8]{1,0:T(4,128)} custom-call(f32[256,128]{1,0:T(8,128)S(1)} %bitcast.10), custom_call_target="tpu_custom_call" | custom-call | tf_op jit(solution)/shard_map/power/pallas_call | solution.py:318
Async XLA Ops:
  30.7 15.2 %all-to-all-start.1 = ((f32[128,4,128]{2,1,0:T(4,128)}), f32[128,4,128]{2,1,0:T(4,128)S(1)}, u32[]{:S(2)}, u32[]{:S(2)}) async-start(f32[128,4,128]{2,1,0:T(4,128)} %bitcast.3), calls=%async_computation.1 | async-start | bytes 524288 | tf_op jit(solution)/shard_map/all_to_all | solution.py:327
  34.5 11.3 %copy-start = (f32[8,128]{1,0:T(8,128)S(1)}, f32[8,128]{1,0:T(8,128)}, u32[]{:S(2)}) copy-start(f32[8,128]{1,0:T(8,128)} %constant.2.clone.start_ref) | copy-start | bytes 12292

commit v3 on v2

--- a/solution.py
+++ b/solution.py
@@ -17,9 +17,10 @@
 SAMPLES = 16384
 DEVICES = 128
 LOCAL = 256
-STEP_CHUNKS = 8
-STEP_ROWS = NFFT * STEP_CHUNKS
-STEPS = SAMPLES // STEP_ROWS
+CHUNKS = SAMPLES // NFFT
+PIECES = (20, 32, 12)
+AHEAD = 2
+PAIR = 2
 AXES = ("wide", "narrow")
 NT = (((1,), (1,)), ((), ()))
 NN = (((1,), (0,)), ((), ()))
@@ -38,24 +39,24 @@
 
 def gram_kernel(
     starts_hbm, bins_hbm, weights_hbm, pressure_hbm, gram_ref, high_ref, low_ref,
-    starts_ref, bins_ref, weights_ref, pressure_ref, q_ref, small_sems, sems,
+    starts_ref, bins_ref, weights_ref, pressure_ref, rows_ref, q_ref, small_sems, sems,
 ):
     small = [
         pltpu.make_async_copy(starts_hbm, starts_ref, small_sems.at[0]),
         pltpu.make_async_copy(bins_hbm, bins_ref, small_sems.at[1]),
         pltpu.make_async_copy(weights_hbm, weights_ref, small_sems.at[2]),
     ]
-
-    def chunk_copy(step):
-        rows = pl.ds(pl.multiple_of(step * STEP_ROWS, STEP_ROWS), STEP_ROWS)
-        return pltpu.make_async_copy(pressure_hbm.at[rows, :], pressure_ref.at[rows, :], sems.at[step])
-
+    copies = []
+    begin = 0
+    for piece, chunks in enumerate(PIECES):
+        rows = slice(begin * NFFT, (begin + chunks) * NFFT)
+        copies.append(pltpu.make_async_copy(pressure_hbm.at[rows, :], pressure_ref.at[rows, :], sems.at[piece]))
+        begin += chunks
     for copy in small:
         copy.start()
-    for step in range(STEPS):
-        chunk_copy(step).start()
-
-    q_ref[...] = jnp.zeros_like(q_ref)
+    for copy in copies[:AHEAD]:
+        copy.start()
+
     row = lax.broadcasted_iota(jnp.int32, (8, NFFT), 0)
     time = lax.broadcasted_iota(jnp.int32, (8, NFFT), 1)
     which = row & 3
@@ -71,39 +72,49 @@
     phase = 2.0 * math.pi * ((bins * time) & (NFFT - 1)).astype(F32) / NFFT
     table = jnp.where(row < 4, scaled * jnp.cos(phase), -scaled * jnp.sin(phase))
     table = table.astype(BF).astype(F32)
-
-    def one_step(step, carry):
-        first = 2 * STEP_CHUNKS * step - 2
-        rolled = []
-        begins = []
-        for k in range(2 * STEP_CHUNKS + 3):
-            block = first + k
-            start = starts_ref[jnp.clip(block, 0, NB - 1)]
-            rolled.append(pltpu.roll(table, start & (NFFT - 1), 1))
-            begins.append(jnp.where((block >= 0) & (block < NB), start, 1 << 20))
-        chunk_copy(step).wait()
-        for c in range(STEP_CHUNKS):
-            base = (step * STEP_CHUNKS + c) * NFFT
-            parts = []
-            for k in range(5):
-                at = time + (base - begins[2 * c + k])
-                parts.append(jnp.where((at >= 0) & (at < NFFT), rolled[2 * c + k], 0.0))
-            parts.append(jnp.zeros((8, NFFT), F32))
-            lhs = jnp.concatenate(parts, 0).astype(BF)
-            rows = pl.ds(pl.multiple_of(base, NFFT), NFFT)
-            got = dot(lhs, pressure_ref[rows, :], NN)
-            rows = pl.ds(pl.multiple_of(step * (16 * STEP_CHUNKS) + 16 * c, 8), 40)
-            q_ref[0, rows, :] += got[:40, :128]
-            q_ref[1, rows, :] += got[:40, 128:]
-        return carry
-
-    lax.fori_loop(0, STEPS, one_step, 0)
+    zero = jnp.zeros((8, NFFT), F32)
+
+    rolled = {}
+    for c in range(CHUNKS):
+        parts = []
+        for block in range(2 * c - 2, 2 * c + 3):
+            if block < 0 or block >= NB:
+                parts.append(zero)
+                continue
+            start = starts_ref[block]
+            if block not in rolled:
+                rolled[block] = pltpu.roll(table, start & (NFFT - 1), 1)
+            at = time + (c * NFFT - start)
+            parts.append(jnp.where((at >= 0) & (at < NFFT), rolled[block], 0.0))
+        parts.append(zero)
+        rows_ref[c] = jnp.concatenate(parts, 0).astype(BF)
+
+    sums = {}
+    begin = 0
+    for piece, chunks in enumerate(PIECES):
+        copies[piece].wait()
+        if piece + AHEAD < len(PIECES):
+            copies[piece + AHEAD].start()
+        for c in range(begin, begin + chunks):
+            got = dot(rows_ref[c], pressure_ref[c * NFFT : (c + 1) * NFFT, :], NN)
+            for k, block in enumerate(range(2 * c - 2, 2 * c + 3)):
+                if 0 <= block < NB:
+                    part = got[8 * k : 8 * k + 8]
+                    sums[block] = sums[block] + part if block in sums else part
+            for block in sorted(sums):
+                if block <= 2 * c - 1 or c == CHUNKS - 1:
+                    done = sums.pop(block)
+                    q_ref[0, 8 * block : 8 * block + 8, :] = done[:, :128]
+                    q_ref[1, 8 * block : 8 * block + 8, :] = done[:, 128:]
+        begin += chunks
+    for h in range(2):
+        q_ref[h, 8 * NB : 8 * NB + 8, :] = jnp.zeros((8, 128), F32)
 
     weights = weights_ref[...]
     upper = lax.broadcasted_iota(jnp.int32, (128, 128), 1) >= lax.broadcasted_iota(jnp.int32, (128, 128), 0)
     for f in range(BINS):
         halves = [
-            jnp.concatenate([q_ref[h, pl.ds(16 + g, 128, stride=8), :] for g in (f, 4 + f)], 0) for h in range(2)
+            jnp.concatenate([q_ref[h, pl.ds(g, 128, stride=8), :] for g in (f, 4 + f)], 0) for h in range(2)
         ]
         both = jnp.concatenate(halves, 1)
         hi, lo = split(both)
@@ -135,9 +146,10 @@
             pltpu.SMEM((BINS,), jnp.int32),
             pltpu.VMEM((1, LOCAL), F32),
             pltpu.VMEM((SAMPLES, LOCAL), BF),
-            pltpu.VMEM((2, 1048, 128), F32),
+            pltpu.VMEM((CHUNKS, 48, NFFT), BF),
+            pltpu.VMEM((2, 1024, 128), F32),
             pltpu.SemaphoreType.DMA((3,)),
-            pltpu.SemaphoreType.DMA((STEPS,)),
+            pltpu.SemaphoreType.DMA((len(PIECES),)),
         ],
         compiler_params=pltpu.CompilerParams(vmem_limit_bytes=24 << 20),
         cost_estimate=pl.CostEstimate(flops=800_000_000, transcendentals=0, bytes_accessed=10_000_000),
@@ -168,26 +180,26 @@
         plow_ref[0, 128:, cols] = plo
 
 
-def project(green_table, high, low):
+def project(green_table, high, low, first):
     return pl.pallas_call(
         project_kernel,
         out_shape=(
-            pltpu.HBM((BINS, 256, MICS), BF),
-            pltpu.HBM((BINS, 256, MICS), BF),
+            pltpu.HBM((PAIR, 256, MICS), BF),
+            pltpu.HBM((PAIR, 256, MICS), BF),
         ),
-        grid=(BINS,),
+        grid=(PAIR,),
         in_specs=[
-            pl.BlockSpec((1, 2, MICS, 128), lambda f: (f, 0, 0, 0)),
-            pl.BlockSpec((1, 2, MICS, 128), lambda f: (f, 0, 0, 1)),
-            pl.BlockSpec((1, 256, LOCAL), lambda f: (f, 0, 0)),
-            pl.BlockSpec((1, 256, LOCAL), lambda f: (f, 0, 0)),
+            pl.BlockSpec((1, 2, MICS, 128), lambda f: (first + f, 0, 0, 0)),
+            pl.BlockSpec((1, 2, MICS, 128), lambda f: (first + f, 0, 0, 1)),
+            pl.BlockSpec((1, 256, LOCAL), lambda f: (first + f, 0, 0)),
+            pl.BlockSpec((1, 256, LOCAL), lambda f: (first + f, 0, 0)),
         ],
         out_specs=[
             pl.BlockSpec((1, 256, MICS), lambda f: (f, 0, 0)),
             pl.BlockSpec((1, 256, MICS), lambda f: (f, 0, 0)),
         ],
         compiler_params=pltpu.CompilerParams(vmem_limit_bytes=24 << 20),
-        cost_estimate=pl.CostEstimate(flops=3_300_000_000, transcendentals=0, bytes_accessed=14_000_000),
+        cost_estimate=pl.CostEstimate(flops=1_650_000_000, transcendentals=0, bytes_accessed=7_000_000),
         name="project",
     )(in_hbm(green_table), in_hbm(green_table), high, low)
 
@@ -210,11 +222,12 @@
     )(parts)
 
 
-def modes_kernel(gram_ref, start_ref, phigh_hbm, plow_hbm, out_ref, phigh_ref, plow_ref, sems):
-    fetch = [
-        pltpu.make_async_copy(phigh_hbm, phigh_ref, sems.at[0]),
-        pltpu.make_async_copy(plow_hbm, plow_ref, sems.at[1]),
-    ]
+def modes_kernel(gram_ref, start_ref, high01, low01, high23, low23, out_ref, phigh_ref, plow_ref, sems):
+    fetch = []
+    for pair, (high, low) in enumerate(((high01, low01), (high23, low23))):
+        place = slice(PAIR * pair, PAIR * pair + PAIR)
+        fetch.append(pltpu.make_async_copy(high, phigh_ref.at[place], sems.at[2 * pair]))
+        fetch.append(pltpu.make_async_copy(low, plow_ref.at[place], sems.at[2 * pair + 1]))
     for copy in fetch:
         copy.start()
     col = lax.broadcasted_iota(jnp.int32, (128, 128), 1)
@@ -280,19 +293,19 @@
     return jnp.asarray(basis)
 
 
-def amplitudes(gram, phigh, plow):
+def amplitudes(gram, projected):
     return pl.pallas_call(
         modes_kernel,
         out_shape=jax.ShapeDtypeStruct((2 * DEVICES, 128), F32),
-        in_specs=[pl.BlockSpec(memory_space=pltpu.VMEM)] * 2 + [pl.BlockSpec(memory_space=pltpu.HBM)] * 2,
+        in_specs=[pl.BlockSpec(memory_space=pltpu.VMEM)] * 2 + [pl.BlockSpec(memory_space=pltpu.HBM)] * 4,
         scratch_shapes=[
             pltpu.VMEM((BINS, 256, MICS), BF),
             pltpu.VMEM((BINS, 256, MICS), BF),
-            pltpu.SemaphoreType.DMA((2,)),
+            pltpu.SemaphoreType.DMA((4,)),
         ],
         compiler_params=pltpu.CompilerParams(vmem_limit_bytes=24 << 20),
         name="modes",
-    )(gram, start_basis(), in_hbm(phigh), in_hbm(plow))
+    )(gram, start_basis(), *[in_hbm(x) for x in projected])
 
 
 def power_kernel(parts_ref, out_ref):
@@ -330,10 +343,13 @@
 def on_device(pressure, weights, green_table, starts, bin_index):
     gram, high, low = local_gram(pressure, weights, starts, bin_index)
     parts = exchange(gram.reshape(DEVICES, 4, 128))
-    phigh, plow = project(green_table, high, low)
+    early = project(green_table, high, low, 0)
+    parts, early = lax.optimization_barrier((parts, early))
     shared = share_sum(parts.reshape(512, 128))
+    shared, high, low = lax.optimization_barrier((shared, high, low))
     summed = exchange(shared.reshape(DEVICES, 4, 128)).reshape(512, 128)
-    partial = amplitudes(summed, phigh, plow)
+    late = project(green_table, high, low, PAIR)
+    partial = amplitudes(summed, (*early, *late))
     return power(exchange(partial.reshape(DEVICES, 2, 128)).reshape(2 * DEVICES, 128))
 
 

time: 68.3 us -> 64.4 us (0.943)
  blocking collectives: 39.2 us -> 13.9 us
  starting transfers between devices: 3.87 us -> 15.4 us
  waiting for transfers between devices: 3.27 us -> 13 us
    all_to_all x2 -> x1, blocking collectives: 39.2 us -> 13.9 us  [exchange(): return lax.all_to_all(x, AXES, 0, 0, tiled=True)]
    all_to_all x1 -> x2, starting transfers between devices: 3.87 us -> 15.4 us  [exchange(): return lax.all_to_all(x, AXES, 0, 0, tiled=True)]
    all_to_all x1 -> x2, waiting for transfers between devices: 3.27 us -> 13 us  [exchange(): return lax.all_to_all(x, AXES, 0, 0, tiled=True)]
    pallas_call x1, Pallas kernels: 7.25 us -> 5.68 us  [local_gram(): pl.pallas_call(gram_kernel, out_shape=(jax.ShapeDtypeStruct((BINS * 128,...]
    pallas_call x1 -> x2, Pallas kernels: 8.04 us -> 9.61 us  [project(): pl.pallas_call(project_kernel, out_shape=(pltpu.HBM((PAIR, 256, MICS), BF...]
  transfers between devices with their start and end apart: 1 -> 2, of which waited for: 1 -> 2; matrix products, arithmetic and copies ran while one was open for 0% -> 0% of each run, Pallas kernels for 12% -> 15%
where the time goes in v3:
time: 64.4 us; the launch traced here: 64.1 us
  Pallas kernels  21.7 us (34%)
  starting transfers between devices  15.4 us (24%)
  blocking collectives  13.9 us (22%)
  waiting for transfers between devices  13 us (20%)
    all_to_all x2, starting transfers between devices, exchange(): return lax.all_to_all(x, AXES, 0, 0, tiled=True)  15.4 us
    all_to_all x1, blocking collectives, exchange(): return lax.all_to_all(x, AXES, 0, 0, tiled=True)  13.9 us
    all_to_all x2, waiting for transfers between devices, exchange(): return lax.all_to_all(x, AXES, 0, 0, tiled=True)  13 us
    pallas_call x2, Pallas kernels, project(): pl.pallas_call(project_kernel, out_shape=(pltpu.HBM((PAIR, 256, MICS), BF...  9.61 us
    pallas_call x1, Pallas kernels, local_gram(): pl.pallas_call(gram_kernel, out_shape=(jax.ShapeDtypeStruct((BINS * 128,...  5.68 us
    pallas_call x1, Pallas kernels, amplitudes(): pl.pallas_call(modes_kernel, out_shape=jax.ShapeDtypeStruct((2 * DEVICES,...  4.97 us
  transfers between devices with their start and end apart: 2, of which 2 were waited for; matrix products, arithmetic and copies ran while one was open for 0% of the time, Pallas kernels for 15%

profile of v3, /device:TPU:1, one launch (start us, length us, event | category | flops | bytes accessed | tf_op | source)
XLA Modules:
  0.0 64.1 jit_solution(17181990534259253103)
XLA Ops:
  0.0 5.7 %gram.1 = (f32[512,128]{1,0:T(8,128)}, bf16[4,256,256]{2,1,0:T(8,128)(2,1)S(1)}, bf16[4,256,256]{2,1,0:T(8,128)(2,1)S(1)}) custom-call(s32[127]{0:T(128)} %starts_hbm.1, s32[4]{0:T(128)} %bins_hbm.1, f32[1,256]{1,0:T(1,128)} %bitcast.12, bf16[16384,256]{1,0:T(8,128)(2,1)} %pressure_hbm.1), custom_call_target="tpu_custom_call" | custom-call | flops 800000000 | bytes 10000000 | tf_op jit(solution)/shard_map/gram/pallas_call | solution.py:136
  5.7 11.5 %all-to-all-start = ((f32[128,4,128]{2,1,0:T(4,128)}), f32[128,4,128]{2,1,0:T(4,128)S(1)}, u32[]{:S(2)}, u32[]{:S(2)}) async-start(f32[128,4,128]{2,1,0:T(4,128)} %bitcast.1), calls=%async_computation | async-start | bytes 524288 | tf_op jit(solution)/shard_map/all_to_all | solution.py:340
  17.2 4.8 %project.2 = (bf16[2,256,1024]{2,1,0:T(8,128)(2,1)}, bf16[2,256,1024]{2,1,0:T(8,128)(2,1)}) custom-call(f32[4,2,1024,256]{3,2,1,0:T(8,128)} %right_ref.3, f32[4,2,1024,256]{3,2,1,0:T(8,128)} %right_ref.3, bf16[4,256,256]{2,1,0:T(8,128)(2,1)S(1)} %get-tuple-element.27.high_ref, bf16[4,256,256]{2,1,0:T(8,128)(2,1)S(1)} %get-tuple-element.28.low_ref), custom_call_target="tpu_custom_call" | custom-call | flops 1650000000 | bytes 7000000 | tf_op jit(solution)/shard_map/project/pallas_call | solution.py:184
  22.0 6.5 %all-to-all-done = f32[128,4,128]{2,1,0:T(4,128)S(1)} async-done(((f32[128,4,128]{2,1,0:T(4,128)}), f32[128,4,128]{2,1,0:T(4,128)S(1)}, u32[]{:S(2)}, u32[]{:S(2)}) %all-to-all-start) | async-done | bytes 262176 | tf_op jit(solution)/shard_map/all_to_all | solution.py:340
  28.5 0.8 %share.1 = f32[512,128]{1,0:T(8,128)} custom-call(f32[512,128]{1,0:T(8,128)S(1)} %bitcast.8), custom_call_target="tpu_custom_call" | custom-call | tf_op jit(solution)/shard_map/share/pallas_call | solution.py:217
  29.3 3.9 %all-to-all-start.1 = ((f32[128,4,128]{2,1,0:T(4,128)}), f32[128,4,128]{2,1,0:T(4,128)S(1)}, u32[]{:S(2)}, u32[]{:S(2)}) async-start(f32[128,4,128]{2,1,0:T(4,128)} %bitcast.3), calls=%async_computation.1 | async-start | bytes 524288 | tf_op jit(solution)/shard_map/all_to_all | solution.py:340
  33.2 0.0 copy-start
  33.2 4.8 %project.3 = (bf16[2,256,1024]{2,1,0:T(8,128)(2,1)}, bf16[2,256,1024]{2,1,0:T(8,128)(2,1)}) custom-call(f32[4,2,1024,256]{3,2,1,0:T(8,128)} %right_ref.3, f32[4,2,1024,256]{3,2,1,0:T(8,128)} %right_ref.3, bf16[4,256,256]{2,1,0:T(8,128)(2,1)S(1)} %get-tuple-element.27.high_ref, bf16[4,256,256]{2,1,0:T(8,128)(2,1)S(1)} %get-tuple-element.28.low_ref), custom_call_target="tpu_custom_call" | custom-call | flops 1650000000 | bytes 7000000 | tf_op jit(solution)/shard_map/project/pallas_call | solution.py:184
  38.0 6.5 %all-to-all-done.1 = f32[128,4,128]{2,1,0:T(4,128)S(1)} async-done(((f32[128,4,128]{2,1,0:T(4,128)}), f32[128,4,128]{2,1,0:T(4,128)S(1)}, u32[]{:S(2)}, u32[]{:S(2)}) %all-to-all-start.1) | async-done | bytes 262176 | tf_op jit(solution)/shard_map/all_to_all | solution.py:340
  44.5 0.0 copy-done
  44.5 5.0 %modes.1 = f32[256,128]{1,0:T(8,128)S(1)} custom-call(f32[512,128]{1,0:T(8,128)S(1)} %bitcast.9, f32[8,128]{1,0:T(8,128)S(1)} %copy-done, bf16[2,256,1024]{2,1,0:T(8,128)(2,1)} %get-tuple-element.25.high01, bf16[2,256,1024]{2,1,0:T(8,128)(2,1)} %get-tuple-element.26.low01, bf16[2,256,1024]{2,1,0:T(8,128)(2,1)} %get-tuple-element.29.high23, ...), custom_call_target="tpu_custom_call" | custom-call | tf_op jit(solution)/shard_map/modes/pallas_call | solution.py:297
  49.5 13.9 %all_to_all.15 = f32[128,2,128]{2,1,0:T(2,128)S(1)} all-to-all(f32[128,2,128]{2,1,0:T(2,128)S(1)} %bitcast.11), channel_id=1, replica_groups=mesh['wide'=32,'narrow'=4] {'wide','narrow'}, dimensions={0} | all-to-all | bytes 262144 | tf_op jit(solution)/shard_map/all_to_all | solution.py:340
  63.4 0.7 %power.1 = f32[4,8]{1,0:T(4,128)} custom-call(f32[256,128]{1,0:T(8,128)S(1)} %bitcast.10), custom_call_target="tpu_custom_call" | custom-call | tf_op jit(solution)/shard_map/power/pallas_call | solution.py:331
Async XLA Ops:
  5.7 22.8 %all-to-all-start = ((f32[128,4,128]{2,1,0:T(4,128)}), f32[128,4,128]{2,1,0:T(4,128)S(1)}, u32[]{:S(2)}, u32[]{:S(2)}) async-start(f32[128,4,128]{2,1,0:T(4,128)} %bitcast.1), calls=%async_computation | async-start | bytes 524288 | tf_op jit(solution)/shard_map/all_to_all | solution.py:340
  29.3 15.2 %all-to-all-start.1 = ((f32[128,4,128]{2,1,0:T(4,128)}), f32[128,4,128]{2,1,0:T(4,128)S(1)}, u32[]{:S(2)}, u32[]{:S(2)}) async-start(f32[128,4,128]{2,1,0:T(4,128)} %bitcast.3), calls=%async_computation.1 | async-start | bytes 524288 | tf_op jit(solution)/shard_map/all_to_all | solution.py:340
  33.2 11.3 %copy-start = (f32[8,128]{1,0:T(8,128)S(1)}, f32[8,128]{1,0:T(8,128)}, u32[]{:S(2)}) copy-start(f32[8,128]{1,0:T(8,128)} %constant.2.clone.start_ref) | copy-start | bytes 12292

commit v4 on v3

--- a/solution.py
+++ b/solution.py
@@ -13,6 +13,7 @@
 BINS = 4
 MODES = 4
 ITERS = 8
+KEPT = 0.01
 MICS = 1024
 SAMPLES = 16384
 DEVICES = 128
@@ -222,7 +223,58 @@
     )(parts)
 
 
-def modes_kernel(gram_ref, start_ref, high01, low01, high23, low23, out_ref, phigh_ref, plow_ref, sems):
+def row(x, index):
+    return jnp.broadcast_to(x[index : index + 1, :], (8, 128))
+
+
+def lane_sum(x):
+    return jnp.broadcast_to(jnp.sum(x, axis=1, keepdims=True), (8, 128))
+
+
+def by_columns(y, turned, later, here):
+    for j in range(MODES):
+        vre, vim = row(y, j), row(y, 4 + j)
+        inverse = lax.rsqrt(lane_sum(vre * vre + vim * vim) + 1e-06)
+        scale = inverse if j == 0 else jnp.where(here[j], inverse, scale)
+        if j < MODES - 1:
+            square = jnp.where(later[j], inverse * inverse, 0.0)
+            coef = lane_sum(y * vre + turned * vim) * square
+            cross = lane_sum(y * vim - turned * vre) * square
+            y, turned = y - (coef * vre + cross * vim), turned - (coef * vim - cross * vre)
+    return (y, turned), scale
+
+
+def by_products(y, turned, later, here):
+    coefs, crosses = [], []
+    for j in range(MODES):
+        vre, vim = row(y, j), row(y, 4 + j)
+        coefs.append(lane_sum(y * vre + turned * vim))
+        crosses.append(lane_sum(y * vim - turned * vre) if j < MODES - 1 else None)
+    whole = [row(coefs[j], j) * KEPT for j in range(MODES)]
+    sound = None
+    for j in range(MODES):
+        norm = row(coefs[j], j)
+        kept = jnp.where(norm >= whole[j], 1.0, 0.0)
+        sound = kept if j == 0 else jnp.minimum(sound, kept)
+        inverse = lax.rsqrt(norm + 1e-06)
+        scale = inverse if j == 0 else jnp.where(here[j], inverse, scale)
+        if j < MODES - 1:
+            square = inverse * inverse
+            twice = square * (2.0 - square * norm)
+            coef, cross = coefs[j], crosses[j]
+            for i in range(j + 1, MODES):
+                are, aim = row(coef, i) * twice, row(coef, 4 + i) * twice
+                coefs[i] = coefs[i] - (are * coef - aim * cross)
+                if i < MODES - 1:
+                    crosses[i] = crosses[i] - (are * cross + aim * coef)
+            square = jnp.where(later[j], square, 0.0)
+            coef, cross = coef * square, cross * square
+            vre, vim = row(y, j), row(y, 4 + j)
+            y, turned = y - (coef * vre + cross * vim), turned - (coef * vim - cross * vre)
+    return (y, turned), scale, sound
+
+
+def modes_kernel(gram_ref, start_ref, high01, low01, high23, low23, out_ref, phigh_ref, plow_ref, mats_ref, sems):
     fetch = []
     for pair, (high, low) in enumerate(((high01, low01), (high23, low23))):
         place = slice(PAIR * pair, PAIR * pair + PAIR)
@@ -234,55 +286,61 @@
     row = lax.broadcasted_iota(jnp.int32, (128, 128), 0)
     lane_row = lax.broadcasted_iota(jnp.int32, (8, 128), 0)
     sign = jnp.where(lane_row < 4, 1.0, -1.0)
-    mats = []
+    mode = lane_row & 3
+    later = [mode > j for j in range(MODES)]
+    here = [mode == j for j in range(MODES)]
     for f in range(BINS):
         packed = gram_ref[f * 128 : (f + 1) * 128, :]
         flipped = packed.T
         gram_re = jnp.where(col >= row, packed, flipped)
         gram_im = jnp.where(col < row, packed, jnp.where(col > row, -flipped, 0.0))
-        mats.append(split(jnp.concatenate([gram_re, gram_im], 1)))
-    vecs = [start_ref[...]] * BINS
-    for _ in range(ITERS):
-        images = []
+        mats_ref[f, 0], mats_ref[f, 1] = split(jnp.concatenate([gram_re, gram_im], 0))
+    start = start_ref[...]
+
+    def iterate(fast):
+        vecs = [(start, sign * pltpu.roll(start, 4, 0))] * BINS
+        sound = jnp.ones((8, 128), F32)
+        for _ in range(ITERS):
+            pairs = []
+            for f in range(BINS):
+                hi, lo = split(jnp.concatenate(vecs[f], 1))
+                ghi, glo = mats_ref[f, 0], mats_ref[f, 1]
+                prod = dot(jnp.concatenate([hi, lo], 0), ghi, NN)
+                image = prod[:8] + prod[8:] + dot(hi, glo, NN)
+                pairs.append((image, sign * pltpu.roll(image, 4, 0)))
+            vecs = []
+            for f in range(BINS):
+                if fast:
+                    (y, turned), scale, kept = by_products(*pairs[f], later, here)
+                    sound = jnp.minimum(sound, kept)
+                else:
+                    (y, turned), scale = by_columns(*pairs[f], later, here)
+                vecs.append((y * scale, turned * scale))
+        return vecs, sound
+
+    def finish(vecs):
+        amps = []
         for f in range(BINS):
-            hi, lo = split(vecs[f])
-            ghi, glo = mats[f]
-            stacked = jnp.concatenate([hi, lo], 0)
-            prod = dot(stacked, ghi, NN)
-            prod = prod[:8] + prod[8:] + dot(hi, glo, NN)
-            swapped = pltpu.roll(prod[:, 128:], 4, 0)
-            images.append(prod[:, :128] + sign * swapped)
-        for j in range(MODES):
-            for f in range(BINS):
-                y = images[f]
-                vre = y[j : j + 1, :]
-                vim = y[4 + j : 5 + j, :]
-                turned = sign * pltpu.roll(y, 4, 0)
-                coef = jnp.sum(y * vre + turned * vim, axis=1, keepdims=True)
-                inverse = lax.rsqrt(coef[j : j + 1, :] + 1e-06)
-                coef = jnp.broadcast_to(coef, (8, 128))
-                scaled = coef * (inverse * inverse)
-                cross = -sign * pltpu.roll(scaled, 4, 0)
-                later = (lane_row & 3) > j
-                here = (lane_row & 3) == j
-                left = y - (scaled * vre + cross * vim)
-                images[f] = jnp.where(later, left, jnp.where(here, y * inverse, y))
-        vecs = images
+            y, turned = vecs[f]
+            hi, lo = split(jnp.concatenate([y, -turned], 1))
+            prod = dot(jnp.concatenate([hi, lo], 0), phigh_ref[f], NN)
+            amps.append(prod[:8] + prod[8:] + dot(hi, plow_ref[f], NN))
+        for half in range(2):
+            rows = []
+            for i in range(4 * half, 4 * half + 4):
+                for f in range(BINS):
+                    rows.append(amps[f][:, i * 128 : (i + 1) * 128])
+            out_ref[pl.ds(half, 128, stride=2), :] = jnp.concatenate(rows, 0).T
+
+    vecs, sound = iterate(True)
+    is_sound = jnp.min(sound) > 0.5
     for copy in fetch:
         copy.wait()
-    amps = []
-    for f in range(BINS):
-        y = vecs[f]
-        turned = -sign * pltpu.roll(y, 4, 0)
-        hi, lo = split(jnp.concatenate([y, turned], 1))
-        prod = dot(jnp.concatenate([hi, lo], 0), phigh_ref[f], NN)
-        amps.append(prod[:8] + prod[8:] + dot(hi, plow_ref[f], NN))
-    for half in range(2):
-        rows = []
-        for i in range(4 * half, 4 * half + 4):
-            for f in range(BINS):
-                rows.append(amps[f][:, i * 128 : (i + 1) * 128])
-        out_ref[pl.ds(half, 128, stride=2), :] = jnp.concatenate(rows, 0).T
+    finish(vecs)
+
+    @pl.when(jnp.logical_not(is_sound))
+    def _():
+        finish(iterate(False)[0])
 
 
 def start_basis():
@@ -301,6 +359,7 @@
         scratch_shapes=[
             pltpu.VMEM((BINS, 256, MICS), BF),
             pltpu.VMEM((BINS, 256, MICS), BF),
+            pltpu.VMEM((BINS, 2, 256, 128), BF),
             pltpu.SemaphoreType.DMA((4,)),
         ],
         compiler_params=pltpu.CompilerParams(vmem_limit_bytes=24 << 20),

time: 64.4 us -> 62.6 us (0.972)
  Pallas kernels: 21.7 us -> 20 us
    pallas_call x1, Pallas kernels: 4.97 us -> 3.24 us  [amplitudes(): pl.pallas_call(modes_kernel, out_shape=jax.ShapeDtypeStruct((2 * DEVICES,...]
where the time goes in v4:
time: 62.6 us; the launch traced here: 62.4 us
  Pallas kernels  20 us (32%)
  starting transfers between devices  15.4 us (25%)
  blocking collectives  13.9 us (22%)
  waiting for transfers between devices  13 us (21%)
    all_to_all x2, starting transfers between devices, exchange(): return lax.all_to_all(x, AXES, 0, 0, tiled=True)  15.4 us
    all_to_all x1, blocking collectives, exchange(): return lax.all_to_all(x, AXES, 0, 0, tiled=True)  13.9 us
    all_to_all x2, waiting for transfers between devices, exchange(): return lax.all_to_all(x, AXES, 0, 0, tiled=True)  13 us
    pallas_call x2, Pallas kernels, project(): pl.pallas_call(project_kernel, out_shape=(pltpu.HBM((PAIR, 256, MICS), BF...  9.61 us
    pallas_call x1, Pallas kernels, local_gram(): pl.pallas_call(gram_kernel, out_shape=(jax.ShapeDtypeStruct((BINS * 128,...  5.68 us
    pallas_call x1, Pallas kernels, amplitudes(): pl.pallas_call(modes_kernel, out_shape=jax.ShapeDtypeStruct((2 * DEVICES,...  3.24 us
  transfers between devices with their start and end apart: 2, of which 2 were waited for; matrix products, arithmetic and copies ran while one was open for 0% of the time, Pallas kernels for 15%

profile of v4, /device:TPU:1, one launch (start us, length us, event | category | flops | bytes accessed | tf_op | source)
XLA Modules:
  0.0 62.4 jit_solution(14298798132483108473)
XLA Ops:
  0.0 5.7 %gram.1 = (f32[512,128]{1,0:T(8,128)}, bf16[4,256,256]{2,1,0:T(8,128)(2,1)S(1)}, bf16[4,256,256]{2,1,0:T(8,128)(2,1)S(1)}) custom-call(s32[127]{0:T(128)} %starts_hbm.1, s32[4]{0:T(128)} %bins_hbm.1, f32[1,256]{1,0:T(1,128)} %bitcast.12, bf16[16384,256]{1,0:T(8,128)(2,1)} %pressure_hbm.1), custom_call_target="tpu_custom_call" | custom-call | flops 800000000 | bytes 10000000 | tf_op jit(solution)/shard_map/gram/pallas_call | solution.py:137
  5.7 11.5 %all-to-all-start = ((f32[128,4,128]{2,1,0:T(4,128)}), f32[128,4,128]{2,1,0:T(4,128)S(1)}, u32[]{:S(2)}, u32[]{:S(2)}) async-start(f32[128,4,128]{2,1,0:T(4,128)} %bitcast.1), calls=%async_computation | async-start | bytes 524288 | tf_op jit(solution)/shard_map/all_to_all | solution.py:399
  17.2 4.8 %project.2 = (bf16[2,256,1024]{2,1,0:T(8,128)(2,1)}, bf16[2,256,1024]{2,1,0:T(8,128)(2,1)}) custom-call(f32[4,2,1024,256]{3,2,1,0:T(8,128)} %right_ref.3, f32[4,2,1024,256]{3,2,1,0:T(8,128)} %right_ref.3, bf16[4,256,256]{2,1,0:T(8,128)(2,1)S(1)} %get-tuple-element.27.high_ref, bf16[4,256,256]{2,1,0:T(8,128)(2,1)S(1)} %get-tuple-element.28.low_ref), custom_call_target="tpu_custom_call" | custom-call | flops 1650000000 | bytes 7000000 | tf_op jit(solution)/shard_map/project/pallas_call | solution.py:185
  22.0 6.5 %all-to-all-done = f32[128,4,128]{2,1,0:T(4,128)S(1)} async-done(((f32[128,4,128]{2,1,0:T(4,128)}), f32[128,4,128]{2,1,0:T(4,128)S(1)}, u32[]{:S(2)}, u32[]{:S(2)}) %all-to-all-start) | async-done | bytes 262176 | tf_op jit(solution)/shard_map/all_to_all | solution.py:399
  28.5 0.8 %share.1 = f32[512,128]{1,0:T(8,128)} custom-call(f32[512,128]{1,0:T(8,128)S(1)} %bitcast.8), custom_call_target="tpu_custom_call" | custom-call | tf_op jit(solution)/shard_map/share/pallas_call | solution.py:218
  29.3 3.9 %all-to-all-start.1 = ((f32[128,4,128]{2,1,0:T(4,128)}), f32[128,4,128]{2,1,0:T(4,128)S(1)}, u32[]{:S(2)}, u32[]{:S(2)}) async-start(f32[128,4,128]{2,1,0:T(4,128)} %bitcast.3), calls=%async_computation.1 | async-start | bytes 524288 | tf_op jit(solution)/shard_map/all_to_all | solution.py:399
  33.2 0.0 copy-start
  33.2 4.8 %project.3 = (bf16[2,256,1024]{2,1,0:T(8,128)(2,1)}, bf16[2,256,1024]{2,1,0:T(8,128)(2,1)}) custom-call(f32[4,2,1024,256]{3,2,1,0:T(8,128)} %right_ref.3, f32[4,2,1024,256]{3,2,1,0:T(8,128)} %right_ref.3, bf16[4,256,256]{2,1,0:T(8,128)(2,1)S(1)} %get-tuple-element.27.high_ref, bf16[4,256,256]{2,1,0:T(8,128)(2,1)S(1)} %get-tuple-element.28.low_ref), custom_call_target="tpu_custom_call" | custom-call | flops 1650000000 | bytes 7000000 | tf_op jit(solution)/shard_map/project/pallas_call | solution.py:185
  38.0 6.5 %all-to-all-done.1 = f32[128,4,128]{2,1,0:T(4,128)S(1)} async-done(((f32[128,4,128]{2,1,0:T(4,128)}), f32[128,4,128]{2,1,0:T(4,128)S(1)}, u32[]{:S(2)}, u32[]{:S(2)}) %all-to-all-start.1) | async-done | bytes 262176 | tf_op jit(solution)/shard_map/all_to_all | solution.py:399
  44.5 0.0 copy-done
  44.5 3.2 %modes.1 = f32[256,128]{1,0:T(8,128)S(1)} custom-call(f32[512,128]{1,0:T(8,128)S(1)} %bitcast.9, f32[8,128]{1,0:T(8,128)S(1)} %copy-done, bf16[2,256,1024]{2,1,0:T(8,128)(2,1)} %get-tuple-element.25.high01, bf16[2,256,1024]{2,1,0:T(8,128)(2,1)} %get-tuple-element.26.low01, bf16[2,256,1024]{2,1,0:T(8,128)(2,1)} %get-tuple-element.29.high23, ...), custom_call_target="tpu_custom_call" | custom-call | tf_op jit(solution)/shard_map/modes/pallas_call | solution.py:355
  47.8 13.9 %all_to_all.15 = f32[128,2,128]{2,1,0:T(2,128)S(1)} all-to-all(f32[128,2,128]{2,1,0:T(2,128)S(1)} %bitcast.11), channel_id=1, replica_groups=mesh['wide'=32,'narrow'=4] {'wide','narrow'}, dimensions={0} | all-to-all | bytes 262144 | tf_op jit(solution)/shard_map/all_to_all | solution.py:399
  61.7 0.7 %power.1 = f32[4,8]{1,0:T(4,128)} custom-call(f32[256,128]{1,0:T(8,128)S(1)} %bitcast.10), custom_call_target="tpu_custom_call" | custom-call | tf_op jit(solution)/shard_map/power/pallas_call | solution.py:390
Async XLA Ops:
  5.7 22.8 %all-to-all-start = ((f32[128,4,128]{2,1,0:T(4,128)}), f32[128,4,128]{2,1,0:T(4,128)S(1)}, u32[]{:S(2)}, u32[]{:S(2)}) async-start(f32[128,4,128]{2,1,0:T(4,128)} %bitcast.1), calls=%async_computation | async-start | bytes 524288 | tf_op jit(solution)/shard_map/all_to_all | solution.py:399
  29.3 15.2 %all-to-all-start.1 = ((f32[128,4,128]{2,1,0:T(4,128)}), f32[128,4,128]{2,1,0:T(4,128)S(1)}, u32[]{:S(2)}, u32[]{:S(2)}) async-start(f32[128,4,128]{2,1,0:T(4,128)} %bitcast.3), calls=%async_computation.1 | async-start | bytes 524288 | tf_op jit(solution)/shard_map/all_to_all | solution.py:399
  33.2 11.3 %copy-start = (f32[8,128]{1,0:T(8,128)S(1)}, f32[8,128]{1,0:T(8,128)}, u32[]{:S(2)}) copy-start(f32[8,128]{1,0:T(8,128)} %constant.2.clone.start_ref) | copy-start | bytes 12292

commit v5 on v4

--- a/solution.py
+++ b/solution.py
@@ -181,13 +181,10 @@
         plow_ref[0, 128:, cols] = plo
 
 
-def project(green_table, high, low, first):
+def project(green_table, high, low, first, shape):
     return pl.pallas_call(
         project_kernel,
-        out_shape=(
-            pltpu.HBM((PAIR, 256, MICS), BF),
-            pltpu.HBM((PAIR, 256, MICS), BF),
-        ),
+        out_shape=(shape((PAIR, 256, MICS), BF), shape((PAIR, 256, MICS), BF)),
         grid=(PAIR,),
         in_specs=[
             pl.BlockSpec((1, 2, MICS, 128), lambda f: (first + f, 0, 0, 0)),
@@ -251,7 +248,7 @@
         coefs.append(lane_sum(y * vre + turned * vim))
         crosses.append(lane_sum(y * vim - turned * vre) if j < MODES - 1 else None)
     whole = [row(coefs[j], j) * KEPT for j in range(MODES)]
-    sound = None
+    steps = []
     for j in range(MODES):
         norm = row(coefs[j], j)
         kept = jnp.where(norm >= whole[j], 1.0, 0.0)
@@ -268,18 +265,22 @@
                 if i < MODES - 1:
                     crosses[i] = crosses[i] - (are * cross + aim * coef)
             square = jnp.where(later[j], square, 0.0)
-            coef, cross = coef * square, cross * square
-            vre, vim = row(y, j), row(y, 4 + j)
-            y, turned = y - (coef * vre + cross * vim), turned - (coef * vim - cross * vre)
-    return (y, turned), scale, sound
-
-
-def modes_kernel(gram_ref, start_ref, high01, low01, high23, low23, out_ref, phigh_ref, plow_ref, mats_ref, sems):
-    fetch = []
-    for pair, (high, low) in enumerate(((high01, low01), (high23, low23))):
-        place = slice(PAIR * pair, PAIR * pair + PAIR)
-        fetch.append(pltpu.make_async_copy(high, phigh_ref.at[place], sems.at[2 * pair]))
-        fetch.append(pltpu.make_async_copy(low, plow_ref.at[place], sems.at[2 * pair + 1]))
+            steps.append((coef * square, cross * square))
+    return steps, scale, sound
+
+
+def apply(steps, scale, y, turned):
+    for j, (coef, cross) in enumerate(steps):
+        vre, vim = row(y, j), row(y, 4 + j)
+        y, turned = y - (coef * vre + cross * vim), turned - (coef * vim - cross * vre)
+    return y * scale, turned * scale
+
+
+def modes_kernel(gram_ref, start_ref, high23, low23, high01_hbm, low01_hbm, out_ref, high01, low01, mats_ref, sems):
+    fetch = [
+        pltpu.make_async_copy(high01_hbm, high01, sems.at[0]),
+        pltpu.make_async_copy(low01_hbm, low01, sems.at[1]),
+    ]
     for copy in fetch:
         copy.start()
     col = lax.broadcasted_iota(jnp.int32, (128, 128), 1)
@@ -297,34 +298,44 @@
         mats_ref[f, 0], mats_ref[f, 1] = split(jnp.concatenate([gram_re, gram_im], 0))
     start = start_ref[...]
 
-    def iterate(fast):
-        vecs = [(start, sign * pltpu.roll(start, 4, 0))] * BINS
+    def image_of(f, vec):
+        hi, lo = split(jnp.concatenate(vec, 1))
+        ghi, glo = mats_ref[f, 0], mats_ref[f, 1]
+        prod = dot(jnp.concatenate([hi, lo], 0), ghi, NN)
+        image = prod[:8] + prod[8:] + dot(hi, glo, NN)
+        return image, sign * pltpu.roll(image, 4, 0)
+
+    first = (start, sign * pltpu.roll(start, 4, 0))
+
+    def iterate_by_columns():
+        vecs = [first] * BINS
+        for _ in range(ITERS):
+            images = [image_of(f, vecs[f]) for f in range(BINS)]
+            vecs = []
+            for y, turned in images:
+                (y, turned), scale = by_columns(y, turned, later, here)
+                vecs.append((y * scale, turned * scale))
+        return vecs
+
+    def iterate_by_products():
+        images = [image_of(f, first) for f in range(BINS)]
         sound = jnp.ones((8, 128), F32)
-        for _ in range(ITERS):
-            pairs = []
-            for f in range(BINS):
-                hi, lo = split(jnp.concatenate(vecs[f], 1))
-                ghi, glo = mats_ref[f, 0], mats_ref[f, 1]
-                prod = dot(jnp.concatenate([hi, lo], 0), ghi, NN)
-                image = prod[:8] + prod[8:] + dot(hi, glo, NN)
-                pairs.append((image, sign * pltpu.roll(image, 4, 0)))
-            vecs = []
-            for f in range(BINS):
-                if fast:
-                    (y, turned), scale, kept = by_products(*pairs[f], later, here)
-                    sound = jnp.minimum(sound, kept)
-                else:
-                    (y, turned), scale = by_columns(*pairs[f], later, here)
-                vecs.append((y * scale, turned * scale))
-        return vecs, sound
+        for sweep in range(ITERS):
+            nexts = [image_of(f, images[f]) for f in range(BINS)] if sweep < ITERS - 1 else images
+            found = [by_products(*images[f], later, here) for f in range(BINS)]
+            for _, _, kept in found:
+                sound = jnp.minimum(sound, kept)
+            images = [apply(steps, scale, *nexts[f]) for f, (steps, scale, _) in enumerate(found)]
+        return images, sound
 
     def finish(vecs):
         amps = []
         for f in range(BINS):
             y, turned = vecs[f]
             hi, lo = split(jnp.concatenate([y, -turned], 1))
-            prod = dot(jnp.concatenate([hi, lo], 0), phigh_ref[f], NN)
-            amps.append(prod[:8] + prod[8:] + dot(hi, plow_ref[f], NN))
+            high_ref, low_ref = (high01, low01) if f < PAIR else (high23, low23)
+            prod = dot(jnp.concatenate([hi, lo], 0), high_ref[f % PAIR], NN)
+            amps.append(prod[:8] + prod[8:] + dot(hi, low_ref[f % PAIR], NN))
         for half in range(2):
             rows = []
             for i in range(4 * half, 4 * half + 4):
@@ -332,7 +343,7 @@
                     rows.append(amps[f][:, i * 128 : (i + 1) * 128])
             out_ref[pl.ds(half, 128, stride=2), :] = jnp.concatenate(rows, 0).T
 
-    vecs, sound = iterate(True)
+    vecs, sound = iterate_by_products()
     is_sound = jnp.min(sound) > 0.5
     for copy in fetch:
         copy.wait()
@@ -340,7 +351,7 @@
 
     @pl.when(jnp.logical_not(is_sound))
     def _():
-        finish(iterate(False)[0])
+        finish(iterate_by_columns())
 
 
 def start_basis():
@@ -351,20 +362,20 @@
     return jnp.asarray(basis)
 
 
-def amplitudes(gram, projected):
+def amplitudes(gram, early, late):
     return pl.pallas_call(
         modes_kernel,
         out_shape=jax.ShapeDtypeStruct((2 * DEVICES, 128), F32),
-        in_specs=[pl.BlockSpec(memory_space=pltpu.VMEM)] * 2 + [pl.BlockSpec(memory_space=pltpu.HBM)] * 4,
+        in_specs=[pl.BlockSpec(memory_space=pltpu.VMEM)] * 4 + [pl.BlockSpec(memory_space=pltpu.HBM)] * 2,
         scratch_shapes=[
-            pltpu.VMEM((BINS, 256, MICS), BF),
-            pltpu.VMEM((BINS, 256, MICS), BF),
+            pltpu.VMEM((PAIR, 256, MICS), BF),
+            pltpu.VMEM((PAIR, 256, MICS), BF),
             pltpu.VMEM((BINS, 2, 256, 128), BF),
-            pltpu.SemaphoreType.DMA((4,)),
+            pltpu.SemaphoreType.DMA((2,)),
         ],
         compiler_params=pltpu.CompilerParams(vmem_limit_bytes=24 << 20),
         name="modes",
-    )(gram, start_basis(), *[in_hbm(x) for x in projected])
+    )(gram, start_basis(), *late, *[in_hbm(x) for x in early])
 
 
 def power_kernel(parts_ref, out_ref):
@@ -402,13 +413,13 @@
 def on_device(pressure, weights, green_table, starts, bin_index):
     gram, high, low = local_gram(pressure, weights, starts, bin_index)
     parts = exchange(gram.reshape(DEVICES, 4, 128))
-    early = project(green_table, high, low, 0)
+    early = project(green_table, high, low, 0, pltpu.HBM)
     parts, early = lax.optimization_barrier((parts, early))
     shared = share_sum(parts.reshape(512, 128))
     shared, high, low = lax.optimization_barrier((shared, high, low))
     summed = exchange(shared.reshape(DEVICES, 4, 128)).reshape(512, 128)
-    late = project(green_table, high, low, PAIR)
-    partial = amplitudes(summed, (*early, *late))
+    late = project(green_table, high, low, PAIR, jax.ShapeDtypeStruct)
+    partial = amplitudes(summed, early, late)
     return power(exchange(partial.reshape(DEVICES, 2, 128)).reshape(2 * DEVICES, 128))
 
 

time: 62.6 us -> 61.9 us (0.989)
  Pallas kernels: 20 us -> 18.3 us
  waiting for transfers between devices: 13 us -> 14 us
    pallas_call x2, Pallas kernels: 9.61 us -> 8.64 us  [project(): pl.pallas_call(project_kernel, out_shape=(shape((PAIR, 256, MICS), BF), s...]
    all_to_all x2, waiting for transfers between devices: 13 us -> 14 us  [exchange(): return lax.all_to_all(x, AXES, 0, 0, tiled=True)]
    pallas_call x1, Pallas kernels: 3.24 us -> 2.51 us  [amplitudes(): pl.pallas_call(modes_kernel, out_shape=jax.ShapeDtypeStruct((2 * DEVICES,...]
  transfers between devices with their start and end apart: 2 -> 2, of which waited for: 2 -> 2; matrix products, arithmetic and copies ran while one was open for 0% -> 0% of each run, Pallas kernels for 15% -> 14%
where the time goes in v5:
time: 61.9 us; the launch traced here: 61.7 us
  Pallas kernels  18.3 us (30%)
  starting transfers between devices  15.4 us (25%)
  waiting for transfers between devices  14 us (23%)
  blocking collectives  13.9 us (22%)
    all_to_all x2, starting transfers between devices, exchange(): return lax.all_to_all(x, AXES, 0, 0, tiled=True)  15.4 us
    all_to_all x2, waiting for transfers between devices, exchange(): return lax.all_to_all(x, AXES, 0, 0, tiled=True)  14 us
    all_to_all x1, blocking collectives, exchange(): return lax.all_to_all(x, AXES, 0, 0, tiled=True)  13.9 us
    pallas_call x2, Pallas kernels, project(): pl.pallas_call(project_kernel, out_shape=(shape((PAIR, 256, MICS), BF), s...  8.64 us
    pallas_call x1, Pallas kernels, local_gram(): pl.pallas_call(gram_kernel, out_shape=(jax.ShapeDtypeStruct((BINS * 128,...  5.68 us
    pallas_call x1, Pallas kernels, amplitudes(): pl.pallas_call(modes_kernel, out_shape=jax.ShapeDtypeStruct((2 * DEVICES,...  2.51 us
  transfers between devices with their start and end apart: 2, of which 2 were waited for; matrix products, arithmetic and copies ran while one was open for 0% of the time, Pallas kernels for 14%

profile of v5, /device:TPU:1, one launch (start us, length us, event | category | flops | bytes accessed | tf_op | source)
XLA Modules:
  0.0 61.7 jit_solution(12242895577663118315)
XLA Ops:
  0.0 5.7 %gram.1 = (f32[512,128]{1,0:T(8,128)}, bf16[4,256,256]{2,1,0:T(8,128)(2,1)S(1)}, bf16[4,256,256]{2,1,0:T(8,128)(2,1)S(1)}) custom-call(s32[127]{0:T(128)} %starts_hbm.1, s32[4]{0:T(128)} %bins_hbm.1, f32[1,256]{1,0:T(1,128)} %bitcast.12, bf16[16384,256]{1,0:T(8,128)(2,1)} %pressure_hbm.1), custom_call_target="tpu_custom_call" | custom-call | flops 800000000 | bytes 10000000 | tf_op jit(solution)/shard_map/gram/pallas_call | solution.py:137
  5.7 11.5 %all-to-all-start = ((f32[128,4,128]{2,1,0:T(4,128)}), f32[128,4,128]{2,1,0:T(4,128)S(1)}, u32[]{:S(2)}, u32[]{:S(2)}) async-start(f32[128,4,128]{2,1,0:T(4,128)} %bitcast.1), calls=%async_computation | async-start | bytes 524288 | tf_op jit(solution)/shard_map/all_to_all | solution.py:410
  17.2 4.8 %project.2 = (bf16[2,256,1024]{2,1,0:T(8,128)(2,1)}, bf16[2,256,1024]{2,1,0:T(8,128)(2,1)}) custom-call(f32[4,2,1024,256]{3,2,1,0:T(8,128)} %right_ref.3, f32[4,2,1024,256]{3,2,1,0:T(8,128)} %right_ref.3, bf16[4,256,256]{2,1,0:T(8,128)(2,1)S(1)} %get-tuple-element.25.high_ref, bf16[4,256,256]{2,1,0:T(8,128)(2,1)S(1)} %get-tuple-element.26.low_ref), custom_call_target="tpu_custom_call" | custom-call | flops 1650000000 | bytes 7000000 | tf_op jit(solution)/shard_map/project/pallas_call | solution.py:185
  22.0 6.5 %all-to-all-done = f32[128,4,128]{2,1,0:T(4,128)S(1)} async-done(((f32[128,4,128]{2,1,0:T(4,128)}), f32[128,4,128]{2,1,0:T(4,128)S(1)}, u32[]{:S(2)}, u32[]{:S(2)}) %all-to-all-start) | async-done | bytes 262176 | tf_op jit(solution)/shard_map/all_to_all | solution.py:410
  28.5 0.8 %share.1 = f32[512,128]{1,0:T(8,128)} custom-call(f32[512,128]{1,0:T(8,128)S(1)} %bitcast.8), custom_call_target="tpu_custom_call" | custom-call | tf_op jit(solution)/shard_map/share/pallas_call | solution.py:215
  29.3 3.9 %all-to-all-start.1 = ((f32[128,4,128]{2,1,0:T(4,128)}), f32[128,4,128]{2,1,0:T(4,128)S(1)}, u32[]{:S(2)}, u32[]{:S(2)}) async-start(f32[128,4,128]{2,1,0:T(4,128)} %bitcast.3), calls=%async_computation.1 | async-start | bytes 524288 | tf_op jit(solution)/shard_map/all_to_all | solution.py:410
  33.2 0.0 copy-start
  33.2 3.8 %project.3 = (bf16[2,256,1024]{2,1,0:T(8,128)(2,1)S(1)}, bf16[2,256,1024]{2,1,0:T(8,128)(2,1)S(1)}) custom-call(f32[4,2,1024,256]{3,2,1,0:T(8,128)} %right_ref.3, f32[4,2,1024,256]{3,2,1,0:T(8,128)} %right_ref.3, bf16[4,256,256]{2,1,0:T(8,128)(2,1)S(1)} %get-tuple-element.25.high_ref, bf16[4,256,256]{2,1,0:T(8,128)(2,1)S(1)} %get-tuple-element.26.low_ref), custom_call_target="tpu_custom_call" | custom-call | flops 1650000000 | bytes 7000000 | tf_op jit(solution)/shard_map/project/pallas_call | solution.py:185
  37.1 7.5 %all-to-all-done.1 = f32[128,4,128]{2,1,0:T(4,128)S(1)} async-done(((f32[128,4,128]{2,1,0:T(4,128)}), f32[128,4,128]{2,1,0:T(4,128)S(1)}, u32[]{:S(2)}, u32[]{:S(2)}) %all-to-all-start.1) | async-done | bytes 262176 | tf_op jit(solution)/shard_map/all_to_all | solution.py:410
  44.5 0.0 copy-done
  44.5 2.5 %modes.1 = f32[256,128]{1,0:T(8,128)S(1)} custom-call(f32[512,128]{1,0:T(8,128)S(1)} %bitcast.9, f32[8,128]{1,0:T(8,128)S(1)} %copy-done, bf16[2,256,1024]{2,1,0:T(8,128)(2,1)S(1)} %get-tuple-element.27.high23, bf16[2,256,1024]{2,1,0:T(8,128)(2,1)S(1)} %get-tuple-element.28.low23, bf16[2,256,1024]{2,1,0:T(8,128)(2,1)} %get-tuple-element.29.high01_hbm, ...), custom_call_target="tpu_custom_call" | custom-call | tf_op jit(solution)/shard_map/modes/pallas_call | solution.py:366
  47.0 13.9 %all_to_all.15 = f32[128,2,128]{2,1,0:T(2,128)S(1)} all-to-all(f32[128,2,128]{2,1,0:T(2,128)S(1)} %bitcast.11), channel_id=1, replica_groups=mesh['wide'=32,'narrow'=4] {'wide','narrow'}, dimensions={0} | all-to-all | bytes 262144 | tf_op jit(solution)/shard_map/all_to_all | solution.py:410
  61.0 0.7 %power.1 = f32[4,8]{1,0:T(4,128)} custom-call(f32[256,128]{1,0:T(8,128)S(1)} %bitcast.10), custom_call_target="tpu_custom_call" | custom-call | tf_op jit(solution)/shard_map/power/pallas_call | solution.py:401
Async XLA Ops:
  5.7 22.8 %all-to-all-start = ((f32[128,4,128]{2,1,0:T(4,128)}), f32[128,4,128]{2,1,0:T(4,128)S(1)}, u32[]{:S(2)}, u32[]{:S(2)}) async-start(f32[128,4,128]{2,1,0:T(4,128)} %bitcast.1), calls=%async_computation | async-start | bytes 524288 | tf_op jit(solution)/shard_map/all_to_all | solution.py:410
  29.3 15.2 %all-to-all-start.1 = ((f32[128,4,128]{2,1,0:T(4,128)}), f32[128,4,128]{2,1,0:T(4,128)S(1)}, u32[]{:S(2)}, u32[]{:S(2)}) async-start(f32[128,4,128]{2,1,0:T(4,128)} %bitcast.3), calls=%async_computation.1 | async-start | bytes 524288 | tf_op jit(solution)/shard_map/all_to_all | solution.py:410
  33.2 11.3 %copy-start = (f32[8,128]{1,0:T(8,128)S(1)}, f32[8,128]{1,0:T(8,128)}, u32[]{:S(2)}) copy-start(f32[8,128]{1,0:T(8,128)} %constant.2.clone.start_ref) | copy-start | bytes 12292
